TPU v7x, 32 devices: a whole 2x2x4 slice. The times are simulated.
32 devices in a mesh: dp: 8 (over z, core), fsdp: 4 (over y, x).
Axes of the slice: x: 2, y: 2, z: 4, core: 2. Of those that a mesh axis runs over, the one named last changes fastest.
Arguments:
- tokens: bfloat16 [32768, 768], P(('dp', 'fsdp')), may hold values from -6 to 6
- segments: int32 [32768], P(('dp', 'fsdp')), may hold values from -1 to 15, as said below
- cotangent: bfloat16 [32768, 768], P(('dp', 'fsdp')), may hold values from -6 to 6
- qkv_weight: bfloat16 [768, 2304], P('fsdp'), may hold values from -0.21875 to 0.21875
- qkv_bias: bfloat16 [2304], P('fsdp'), may hold values from -1.796875 to 1.796875
- out_weight: bfloat16 [768, 768], P('fsdp'), may hold values from -0.875 to 0.875
- out_bias: bfloat16 [768], P('fsdp'), may hold values from -1.796875 to 1.796875
- up_weight: bfloat16 [768, 3072], P('fsdp'), may hold values from -0.21875 to 0.21875
- up_bias: bfloat16 [3072], P('fsdp'), may hold values from -1.796875 to 1.796875
- down_weight: bfloat16 [3072, 768], P('fsdp'), may hold values from -0.109375 to 0.109375
- down_bias: bfloat16 [768], P('fsdp'), may hold values from -1.796875 to 1.796875
- first_gain: bfloat16 [768], P('fsdp'), may hold values from 0.5 to 1.5
- first_shift: bfloat16 [768], P('fsdp'), may hold values from -1.796875 to 1.796875
- second_gain: bfloat16 [768], P('fsdp'), may hold values from 0.5 to 1.5
- second_shift: bfloat16 [768], P('fsdp'), may hold values from -1.796875 to 1.796875
- query_gain: bfloat16 [64], P('fsdp'), may hold values from 0.099609375 to 1.8984375
- key_gain: bfloat16 [64], P('fsdp'), may hold values from 0.099609375 to 1.8984375
Outputs:
- out_tokens: bfloat16 [32768, 768], P(('dp', 'fsdp'))
- tokens_grad: bfloat16 [32768, 768], P(('dp', 'fsdp'))
- qkv_weight_grad: float32 [768, 2304], P('fsdp')
- qkv_bias_grad: float32 [2304], P('fsdp')
- out_weight_grad: float32 [768, 768], P('fsdp')
- out_bias_grad: float32 [768], P('fsdp')
- up_weight_grad: float32 [768, 3072], P('fsdp')
- up_bias_grad: float32 [3072], P('fsdp')
- down_weight_grad: float32 [3072, 768], P('fsdp')
- down_bias_grad: float32 [768], P('fsdp')
- first_gain_grad: float32 [768], P('fsdp')
- first_shift_grad: float32 [768], P('fsdp')
- second_gain_grad: float32 [768], P('fsdp')
- second_shift_grad: float32 [768], P('fsdp')
- query_gain_grad: float32 [64], P('fsdp')
- key_gain_grad: float32 [64], P('fsdp')
Inputs may be any that keep to these rules, and one draw needn't show every extreme that they name: `segments`: within each device's block of 1024 patches, equal ids mark one image; -1 marks padding, whose output and gradient vanish. Half of all blocks hold 4 sequences of four small images of 64 patches each; the others hold one sequence: an image of 576 patches, a second image, then padding.
All inputs are finite; a program needn't handle non-finite values.
Results may differ from a plain program's by a relative error of at most 0.024.
Values may be sent and summed in bfloat16 or wider, within the bound.
A program may use at most 256 MiB of HBM per device.

v0:
```python
import jax
import jax.numpy as jnp
from jax import lax
from jax.sharding import PartitionSpec as P

norm_eps = 1e-06


def layer_norm(value, gain, shift):
    centred = value - jnp.mean(value, axis=-1, keepdims=True)
    scaled = centred * lax.rsqrt(jnp.mean(centred * centred, axis=-1, keepdims=True) + norm_eps)
    return scaled * gain + shift


def head_scale(value, gain):
    centred = value - jnp.mean(value, axis=-1, keepdims=True)
    return (
        centred * lax.rsqrt(jnp.mean(centred * centred, axis=-1, keepdims=True) + norm_eps) * gain
    )


def head_norms(query, keys, query_gain, key_gain):
    return (head_scale(query, query_gain), head_scale(keys, key_gain))


def exact_gelu(value):
    return jax.nn.gelu(value, approximate=False)


def left_product(left, right):
    return lax.dot_general(
        left, right, (((0,), (0,)), ((), ())), preferred_element_type=jnp.float32
    )


def right_product(left, right):
    return lax.dot_general(
        left, right, (((1,), (1,)), ((), ())), preferred_element_type=jnp.float32
    )


def block_scores(query_block, key_low, segment_block, segments):
    scores = (
        jnp.einsum("qhe,khe->hqk", query_block, key_low, preferred_element_type=jnp.float32) * 0.125
    )
    allowed = segment_block[:, None] == segments[None, :]
    return jnp.where(allowed[None], scores, -1e30)


def attend(query_low, key_low, value_low, segments):
    count = query_low.shape[0]
    block = min(512, count)

    def one_block(position):
        query_block = lax.dynamic_slice_in_dim(query_low, position * block, block, 0)
        segment_block = lax.dynamic_slice_in_dim(segments, position * block, block, 0)
        scores = block_scores(query_block, key_low, segment_block, segments)
        top = jnp.max(scores, axis=-1, keepdims=True)
        expo = jnp.exp(scores - top)
        total = jnp.sum(expo, axis=-1, keepdims=True)
        weights = (expo / total).astype(jnp.bfloat16)
        attended = jnp.einsum(
            "hqk,khe->qhe", weights, value_low, preferred_element_type=jnp.float32
        )
        return (attended, (top + jnp.log(total))[..., 0])

    attended, log_total = lax.map(one_block, jnp.arange(count // block, dtype=jnp.int32))
    return (attended.reshape(query_low.shape), log_total)


def attend_back(query_low, key_low, value_low, segments, grad_attended, log_total):
    count = query_low.shape[0]
    block = min(512, count)

    def one_block(carry, item):
        key_grad, value_grad = carry
        position, block_total = item
        query_block = lax.dynamic_slice_in_dim(query_low, position * block, block, 0)
        segment_block = lax.dynamic_slice_in_dim(segments, position * block, block, 0)
        grad_block = lax.dynamic_slice_in_dim(grad_attended, position * block, block, 0)
        scores = block_scores(query_block, key_low, segment_block, segments)
        weights = jnp.exp(scores - block_total[..., None])
        value_grad = value_grad + jnp.einsum(
            "hqk,qhe->khe",
            weights.astype(jnp.bfloat16),
            grad_block,
            preferred_element_type=jnp.float32,
        )
        grad_weights = jnp.einsum(
            "qhe,khe->hqk", grad_block, value_low, preferred_element_type=jnp.float32
        )
        grad_scores = weights * (
            grad_weights - jnp.sum(weights * grad_weights, axis=-1, keepdims=True)
        )
        scores_low = grad_scores.astype(jnp.bfloat16)
        query_grad = 0.125 * jnp.einsum(
            "hqk,khe->qhe", scores_low, key_low, preferred_element_type=jnp.float32
        )
        key_grad = key_grad + 0.125 * jnp.einsum(
            "hqk,qhe->khe", scores_low, query_block, preferred_element_type=jnp.float32
        )
        return ((key_grad, value_grad), query_grad)

    empty = jnp.zeros(key_low.shape, jnp.float32)
    (key_grad, value_grad), query_grad = lax.scan(
        one_block, (empty, empty), (jnp.arange(count // block, dtype=jnp.int32), log_total)
    )
    return (query_grad.reshape(query_low.shape), key_grad, value_grad)


def shards(
    tokens,
    segments,
    cotangent,
    qkv_weight,
    qkv_bias,
    out_weight,
    out_bias,
    up_weight,
    up_bias,
    down_weight,
    down_bias,
    first_gain,
    first_shift,
    second_gain,
    second_shift,
    query_gain,
    key_gain,
):
    gathered = (
        lax.all_gather(qkv_weight, "fsdp", axis=0, tiled=True),
        lax.all_gather(qkv_bias, "fsdp", axis=0, tiled=True),
        lax.all_gather(out_weight, "fsdp", axis=0, tiled=True),
        lax.all_gather(out_bias, "fsdp", axis=0, tiled=True),
        lax.all_gather(up_weight, "fsdp", axis=0, tiled=True),
        lax.all_gather(up_bias, "fsdp", axis=0, tiled=True),
        lax.all_gather(down_weight, "fsdp", axis=0, tiled=True),
        lax.all_gather(down_bias, "fsdp", axis=0, tiled=True),
        lax.all_gather(first_gain, "fsdp", axis=0, tiled=True),
        lax.all_gather(first_shift, "fsdp", axis=0, tiled=True),
        lax.all_gather(second_gain, "fsdp", axis=0, tiled=True),
        lax.all_gather(second_shift, "fsdp", axis=0, tiled=True),
        lax.all_gather(query_gain, "fsdp", axis=0, tiled=True),
        lax.all_gather(key_gain, "fsdp", axis=0, tiled=True),
    )
    (
        qkv_matrix,
        qkv_offset,
        proj_matrix,
        proj_offset,
        up_matrix,
        up_offset,
        down_matrix,
        down_offset,
        gain_first,
        shift_first,
        gain_second,
        shift_second,
        gain_query,
        gain_key,
    ) = gathered
    count = tokens.shape[0]
    width = tokens.shape[1]
    head_size = gain_query.shape[0]
    heads = width // head_size
    float_tokens = tokens.astype(jnp.float32)
    normed_first, first_back = jax.vjp(
        layer_norm, float_tokens, gain_first.astype(jnp.float32), shift_first.astype(jnp.float32)
    )
    normed_low = normed_first.astype(jnp.bfloat16)
    mixed = jnp.dot(normed_low, qkv_matrix, preferred_element_type=jnp.float32) + qkv_offset.astype(
        jnp.float32
    )
    query = mixed[:, :width].reshape(count, heads, head_size)
    keys = mixed[:, width : 2 * width].reshape(count, heads, head_size)
    value_low = mixed[:, 2 * width :].reshape(count, heads, head_size).astype(jnp.bfloat16)
    (query_norm, key_norm), norm_back = jax.vjp(
        head_norms, query, keys, gain_query.astype(jnp.float32), gain_key.astype(jnp.float32)
    )
    query_low = query_norm.astype(jnp.bfloat16)
    key_low = key_norm.astype(jnp.bfloat16)
    attended, log_total = attend(query_low, key_low, value_low, segments)
    attended_low = attended.reshape(count, width).astype(jnp.bfloat16)
    residual = (
        float_tokens
        + jnp.dot(attended_low, proj_matrix, preferred_element_type=jnp.float32)
        + proj_offset.astype(jnp.float32)
    )
    normed_second, second_back = jax.vjp(
        layer_norm, residual, gain_second.astype(jnp.float32), shift_second.astype(jnp.float32)
    )
    second_low = normed_second.astype(jnp.bfloat16)
    hidden = jnp.dot(second_low, up_matrix, preferred_element_type=jnp.float32) + up_offset.astype(
        jnp.float32
    )
    active, gelu_back = jax.vjp(exact_gelu, hidden)
    active_low = active.astype(jnp.bfloat16)
    result = jnp.dot(
        active_low, down_matrix, preferred_element_type=jnp.float32
    ) + down_offset.astype(jnp.float32)
    valid = (segments >= 0)[:, None]
    output = jnp.where(valid, residual + result, 0.0).astype(jnp.bfloat16)
    weights_back = (
        lax.all_gather(qkv_weight, "fsdp", axis=0, tiled=True),
        lax.all_gather(qkv_bias, "fsdp", axis=0, tiled=True),
        lax.all_gather(out_weight, "fsdp", axis=0, tiled=True),
        lax.all_gather(out_bias, "fsdp", axis=0, tiled=True),
        lax.all_gather(up_weight, "fsdp", axis=0, tiled=True),
        lax.all_gather(up_bias, "fsdp", axis=0, tiled=True),
        lax.all_gather(down_weight, "fsdp", axis=0, tiled=True),
        lax.all_gather(down_bias, "fsdp", axis=0, tiled=True),
        lax.all_gather(first_gain, "fsdp", axis=0, tiled=True),
        lax.all_gather(first_shift, "fsdp", axis=0, tiled=True),
        lax.all_gather(second_gain, "fsdp", axis=0, tiled=True),
        lax.all_gather(second_shift, "fsdp", axis=0, tiled=True),
        lax.all_gather(query_gain, "fsdp", axis=0, tiled=True),
        lax.all_gather(key_gain, "fsdp", axis=0, tiled=True),
    )
    qkv_again = weights_back[0]
    proj_again = weights_back[2]
    up_again = weights_back[4]
    down_again = weights_back[6]
    grad_output = jnp.where(valid, cotangent.astype(jnp.float32), 0.0)
    result_low = grad_output.astype(jnp.bfloat16)
    down_grad = left_product(active_low, result_low)
    down_offset_grad = jnp.sum(result_low.astype(jnp.float32), axis=0)
    (grad_hidden,) = gelu_back(right_product(result_low, down_again))
    hidden_low = grad_hidden.astype(jnp.bfloat16)
    up_grad = left_product(second_low, hidden_low)
    up_offset_grad = jnp.sum(hidden_low.astype(jnp.float32), axis=0)
    grad_norm_second, second_gain_grad, second_shift_grad = second_back(
        right_product(hidden_low, up_again)
    )
    grad_residual = grad_output + grad_norm_second
    branch_low = grad_residual.astype(jnp.bfloat16)
    proj_grad = left_product(attended_low, branch_low)
    proj_offset_grad = jnp.sum(branch_low.astype(jnp.float32), axis=0)
    grad_attended = (
        right_product(branch_low, proj_again).astype(jnp.bfloat16).reshape(count, heads, head_size)
    )
    query_grad, key_grad, value_grad = attend_back(
        query_low, key_low, value_low, segments, grad_attended, log_total
    )
    grad_query, grad_keys, query_gain_grad, key_gain_grad = norm_back((query_grad, key_grad))
    grad_mixed = jnp.concatenate(
        [
            grad_query.reshape(count, width),
            grad_keys.reshape(count, width),
            value_grad.reshape(count, width),
        ],
        axis=1,
    ).astype(jnp.bfloat16)
    qkv_grad = left_product(normed_low, grad_mixed)
    qkv_offset_grad = jnp.sum(grad_mixed.astype(jnp.float32), axis=0)
    grad_norm_first, first_gain_grad, first_shift_grad = first_back(
        right_product(grad_mixed, qkv_again)
    )
    grad_input = (grad_residual + grad_norm_first).astype(jnp.bfloat16)
    summed = (
        lax.psum_scatter(
            qkv_grad.astype(jnp.bfloat16), "fsdp", scatter_dimension=0, tiled=True
        ).astype(jnp.float32),
        lax.psum_scatter(
            qkv_offset_grad.astype(jnp.bfloat16), "fsdp", scatter_dimension=0, tiled=True
        ).astype(jnp.float32),
        lax.psum_scatter(
            proj_grad.astype(jnp.bfloat16), "fsdp", scatter_dimension=0, tiled=True
        ).astype(jnp.float32),
        lax.psum_scatter(
            proj_offset_grad.astype(jnp.bfloat16), "fsdp", scatter_dimension=0, tiled=True
        ).astype(jnp.float32),
        lax.psum_scatter(
            up_grad.astype(jnp.bfloat16), "fsdp", scatter_dimension=0, tiled=True
        ).astype(jnp.float32),
        lax.psum_scatter(
            up_offset_grad.astype(jnp.bfloat16), "fsdp", scatter_dimension=0, tiled=True
        ).astype(jnp.float32),
        lax.psum_scatter(
            down_grad.astype(jnp.bfloat16), "fsdp", scatter_dimension=0, tiled=True
        ).astype(jnp.float32),
        lax.psum_scatter(
            down_offset_grad.astype(jnp.bfloat16), "fsdp", scatter_dimension=0, tiled=True
        ).astype(jnp.float32),
        lax.psum_scatter(
            first_gain_grad.astype(jnp.bfloat16), "fsdp", scatter_dimension=0, tiled=True
        ).astype(jnp.float32),
        lax.psum_scatter(
            first_shift_grad.astype(jnp.bfloat16), "fsdp", scatter_dimension=0, tiled=True
        ).astype(jnp.float32),
        lax.psum_scatter(
            second_gain_grad.astype(jnp.bfloat16), "fsdp", scatter_dimension=0, tiled=True
        ).astype(jnp.float32),
        lax.psum_scatter(
            second_shift_grad.astype(jnp.bfloat16), "fsdp", scatter_dimension=0, tiled=True
        ).astype(jnp.float32),
        lax.psum_scatter(
            query_gain_grad.astype(jnp.bfloat16), "fsdp", scatter_dimension=0, tiled=True
        ).astype(jnp.float32),
        lax.psum_scatter(
            key_gain_grad.astype(jnp.bfloat16), "fsdp", scatter_dimension=0, tiled=True
        ).astype(jnp.float32),
    )
    final = (
        lax.psum(summed[0].astype(jnp.bfloat16), "dp").astype(jnp.float32),
        lax.psum(summed[1].astype(jnp.bfloat16), "dp").astype(jnp.float32),
        lax.psum(summed[2].astype(jnp.bfloat16), "dp").astype(jnp.float32),
        lax.psum(summed[3].astype(jnp.bfloat16), "dp").astype(jnp.float32),
        lax.psum(summed[4].astype(jnp.bfloat16), "dp").astype(jnp.float32),
        lax.psum(summed[5].astype(jnp.bfloat16), "dp").astype(jnp.float32),
        lax.psum(summed[6].astype(jnp.bfloat16), "dp").astype(jnp.float32),
        lax.psum(summed[7].astype(jnp.bfloat16), "dp").astype(jnp.float32),
        lax.psum(summed[8].astype(jnp.bfloat16), "dp").astype(jnp.float32),
        lax.psum(summed[9].astype(jnp.bfloat16), "dp").astype(jnp.float32),
        lax.psum(summed[10].astype(jnp.bfloat16), "dp").astype(jnp.float32),
        lax.psum(summed[11].astype(jnp.bfloat16), "dp").astype(jnp.float32),
        lax.psum(summed[12].astype(jnp.bfloat16), "dp").astype(jnp.float32),
        lax.psum(summed[13].astype(jnp.bfloat16), "dp").astype(jnp.float32),
    )
    return (
        output,
        grad_input,
        final[0],
        final[1],
        final[2],
        final[3],
        final[4],
        final[5],
        final[6],
        final[7],
        final[8],
        final[9],
        final[10],
        final[11],
        final[12],
        final[13],
    )


def solution(mesh):
    in_specs = (
        P(("dp", "fsdp"), None),
        P(("dp", "fsdp")),
        P(("dp", "fsdp"), None),
        P("fsdp", None),
        P("fsdp"),
        P("fsdp", None),
        P("fsdp"),
        P("fsdp", None),
        P("fsdp"),
        P("fsdp", None),
        P("fsdp"),
        P("fsdp"),
        P("fsdp"),
        P("fsdp"),
        P("fsdp"),
        P("fsdp"),
        P("fsdp"),
    )
    out_specs = (
        P(("dp", "fsdp"), None),
        P(("dp", "fsdp"), None),
        P("fsdp", None),
        P("fsdp"),
        P("fsdp", None),
        P("fsdp"),
        P("fsdp", None),
        P("fsdp"),
        P("fsdp", None),
        P("fsdp"),
        P("fsdp"),
        P("fsdp"),
        P("fsdp"),
        P("fsdp"),
        P("fsdp"),
        P("fsdp"),
    )
    return jax.shard_map(shards, mesh=mesh, in_specs=in_specs, out_specs=out_specs, check_vma=False)
```

profile of v0, /device:TPU:0, one launch (start us, length us, event | category | flops | bytes accessed | tf_op | source)
XLA Modules:
  0.0 847.7 jit_solution(16748366694479090211)
XLA Ops:
  14.7 19.0 %all-reduce.22 = (bf16[2304]{0:T(1024)(128)(2,1)S(1)}, bf16[768]{0:T(1024)(128)(2,1)S(1)}, bf16[768]{0:T(1024)(128)(2,1)S(1)}, bf16[64]{0:T(256)(128)(2,1)S(1)},...) all-reduce(bf16[2304]{0:T(1024)(128)(2,1)S(1)} %dynamic-update-slic, ...), channel_id=1, replica_groups=mesh['dp'=8,'fsdp'=4] {'fsdp'}, use_global_device_ids=true, to_apply=%add.2 | all-reduce | flops 6272 | bytes 25088
  37.2 7.8 all-gather
  48.5 11.7 %all-gather.6.cloned.1.call-done = bf16[768,2304]{1,0:T(8,128)(2,1)} async-done(((bf16[192,2304]{1,0:T(8,128)(2,1)}), bf16[768,2304]{1,0:T(8,128)(2,1)}) %all-gather.6.cloned.1.call-update) | async-done | bytes 3538960 | tf_op jit(solution)/shard_map/all_gather | solution.py:131
  60.1 6.3 convolution_add_fusion
  88.5 4.1 multiply_convert_fusion.2
  92.6 74.7 %while.27 = (s32[]{:T(128)}, bf16[2,512,12,64]{1,3,2,0:T(8,128)(2,1)}, f32[2,12,512]{2,1,0:T(8,128)S(1)}, s32[2]{0:T(128)S(1)}, s32[1024]{0:T(1024)S(1)}, /*inde...) while((s32[]{:T(128)}, ...), condition=%wide.region_9.10_spmd, body=%wide.region_6.9_spmd.sunk | while | flops 1686628352 | bytes 190286576 | solution.py:67
  94.6 11.5 %fusion.114 = (f32[12,512]{1,0:T(8,128)S(1)}, f32[12,512,1024]{2,1,0:T(8,128)}) fusion(pred[512,1024]{1,0:T(8,128)(4,1)S(1)} %broadcast_compare_fusion.5, bf16[1024,12,64]{0,2,1:T(8,128)(2,1)S(1)} %get-tuple-element.489, bf16[1024,12,64]{0,2,1:T(8,128)(2,1)S(1)} %get-tuple-element.488, s32[]{:T(128)S(6)} %select_n.77), kind=kOutput, calls=%fused_computation.3.clone.1 | convolution fusion | flops 824174592 | bytes 28073988 | tf_op jit(solution)/shard_map/while/body/eval_jaxpr/qhe,khe->hqk/dot_general | solution.py:44
  106.1 12.3 %fusion.115 = f32[12,512]{1,0:T(8,128)S(1)} fusion(f32[12,512,1024]{2,1,0:T(8,128)} %get-tuple-element.444, f32[12,512]{1,0:T(8,128)S(1)} %get-tuple-element.445, pred[512,1024]{1,0:T(8,128)(4,1)S(1)} %broadcast_compare_fusion.5), kind=kLoop, calls=%fused_computation.4.clone.1 | loop fusion | flops 25159680 | bytes 25739264 | tf_op jit(solution)/shard_map/while/body/eval_jaxpr/reduce_sum | solution.py:60
  121.9 8.5 %bitcast_dynamic-update-slice_fusion.4 = bf16[2,512,12,64]{1,3,2,0:T(8,128)(2,1)} fusion(bf16[2,512,12,64]{1,3,2,0:T(8,128)(2,1)} %get-tuple-element.472, s32[]{:T(128)} %get-tuple-element.471, bf16[1024,12,64]{0,2,1:T(8,128)(2,1)S(1)} %copy-done.10, f32[12,512,1024]{2,1,0:T(8,128)S(1)} %copy-done, f32[12,512]{1,0:T(8,128)S(1)} %fusion.115, ...), kind=kOutput, calls=%fused_computation.6.clone.1 | convolution fusion | flops 836763648 | bytes 28885504 | tf_op jit(solution)/shard_map/while/body/eval_jaxpr/hqk,khe->qhe/dot_general | solution.py:62
  132.1 10.7 %fusion.114 = (f32[12,512]{1,0:T(8,128)S(1)}, f32[12,512,1024]{2,1,0:T(8,128)}) fusion(pred[512,1024]{1,0:T(8,128)(4,1)S(1)} %broadcast_compare_fusion.5, bf16[1024,12,64]{0,2,1:T(8,128)(2,1)S(1)} %get-tuple-element.489, bf16[1024,12,64]{0,2,1:T(8,128)(2,1)S(1)} %get-tuple-element.488, s32[]{:T(128)S(6)} %select_n.77), kind=kOutput, calls=%fused_computation.3.clone.1 | convolution fusion | flops 824174592 | bytes 28073988 | tf_op jit(solution)/shard_map/while/body/eval_jaxpr/qhe,khe->hqk/dot_general | solution.py:44
  142.7 12.3 %fusion.115 = f32[12,512]{1,0:T(8,128)S(1)} fusion(f32[12,512,1024]{2,1,0:T(8,128)} %get-tuple-element.444, f32[12,512]{1,0:T(8,128)S(1)} %get-tuple-element.445, pred[512,1024]{1,0:T(8,128)(4,1)S(1)} %broadcast_compare_fusion.5), kind=kLoop, calls=%fused_computation.4.clone.1 | loop fusion | flops 25159680 | bytes 25739264 | tf_op jit(solution)/shard_map/while/body/eval_jaxpr/reduce_sum | solution.py:60
  158.8 8.5 %bitcast_dynamic-update-slice_fusion.4 = bf16[2,512,12,64]{1,3,2,0:T(8,128)(2,1)} fusion(bf16[2,512,12,64]{1,3,2,0:T(8,128)(2,1)} %get-tuple-element.472, s32[]{:T(128)} %get-tuple-element.471, bf16[1024,12,64]{0,2,1:T(8,128)(2,1)S(1)} %copy-done.10, f32[12,512,1024]{2,1,0:T(8,128)S(1)} %copy-done, f32[12,512]{1,0:T(8,128)S(1)} %fusion.115, ...), kind=kOutput, calls=%fused_computation.6.clone.1 | convolution fusion | flops 836763648 | bytes 28885504 | tf_op jit(solution)/shard_map/while/body/eval_jaxpr/hqk,khe->qhe/dot_general | solution.py:62
  178.8 4.3 copy.88
  188.7 38.1 %multiply_convert_fusion.1 = (bf16[1024,3072]{1,0:T(8,128)(2,1)}, f32[1024,3072]{1,0:T(8,128)}, f32[1024,3072]{1,0:T(8,128)}) fusion(f32[3072]{0:T(1024)S(1)} %bitcast.137, bf16[768,3072]{1,0:T(8,128)(2,1)} %all-gather.10.cloned.1.call-done, f32[1024,768]{0,1:T(8,128)} %copy-done.14, f32[768]{0:T(1024)S(1)} %copy-done.81, f32[768]{0:T(1024)S(1)} %copy-done.63, ...), kind=kOutput, calls=%fused_computation.40 | convolution fusion | flops 5043388416 | bytes 39348224 | tf_op jit(solution)/shard_map/dot_general | solution.py:193
  226.9 19.2 %fusion.72 = (bf16[3072]{0:T(1024)(128)(2,1)}, bf16[1024,3072]{1,0:T(8,128)(2,1)}) fusion(f32[1024,3072]{1,0:T(8,128)} %get-tuple-element.310, bf16[3072,768]{1,0:T(8,128)(2,1)} %all-gather.12.cloned.1.call-done, bf16[1024,768]{0,1:T(8,128)(2,1)} %copy.84, pred[1024]{0:T(1024)(128)(4,1)S(1)} %copy-done.69, f32[1024,3072]{1,0:T(8,128)} %get-tuple-element.326, ...), kind=kOutput, calls=%fused_computation.139 | convolution fusion | flops 4884526080 | bytes 37768192 | tf_op jit(solution)/shard_map/dot_general | solution.py:37
  246.1 10.3 %fusion.74 = (bf16[768]{0:T(1024)(128)(2,1)}, f32[1024,768]{1,0:T(8,128)}) fusion(bf16[1024,3072]{1,0:T(8,128)(2,1)} %get-tuple-element.328, bf16[768,3072]{1,0:T(8,128)(2,1)} %all-gather.10.cloned.1.call-done), kind=kOutput, calls=%fused_computation.141 | convolution fusion | flops 4832623616 | bytes 14157312 | tf_op jit(solution)/shard_map/dot_general | solution.py:37
  259.9 4.5 multiply_reduce_fusion.3
  270.3 232.9 %while.28 = (s32[]{:T(128)}, f32[1024,12,64]{0,2,1:T(8,128)}, f32[1024,12,64]{0,2,1:T(8,128)}, f32[2,512,12,64]{1,0,3,2:T(2,128)}, s32[2]{0:T(128)S(1)}, /*index...) while((s32[]{:T(128)}, f32[1024,12,64]{0,2,1:T(8,128)}, ...), condition=%wide.region_16.17_spmd.clone, body=%wide.region_14.16_spmd.clone.sunk | while | flops 4125747200 | bytes 242411920 | solution.py:105
  272.1 10.1 %fusion.125 = f32[12,512,1024]{2,1,0:T(8,128)} fusion(bf16[1024,12,64]{0,2,1:T(8,128)(2,1)S(1)} %get-tuple-element.532, bf16[1024,12,64]{0,2,1:T(8,128)(2,1)S(1)} %get-tuple-element.530, s32[]{:T(128)S(6)} %select_n.81), kind=kOutput, calls=%fused_computation.28.clone.1 | convolution fusion | flops 805306368 | bytes 27525124 | tf_op jit(solution)/shard_map/while/body/eval_jaxpr/qhe,khe->hqk/dot_general | solution.py:44
  282.7 18.3 %multiply_reduce_fusion.11 = (f32[12,512]{1,0:T(8,128)S(1)}, f32[12,512,1024]{2,1,0:T(8,128)}) fusion(f32[12,512,1024]{2,1,0:T(8,128)} %fusion.125, f32[12,512]{1,0:T(8,128)S(1)} %dynamic-slice_bitcast_fusion.2, pred[512,1024]{1,0:T(8,128)(4,1)S(1)} %broadcast_compare_fusion.6, bf16[1024,12,64]{0,2,1:T(8,128)(2,1)} %get-tuple-element.535, ...), kind=kOutput, calls=%fused_computation.15.clone.1 | convolution fusion | flops 836757504 | bytes 53264388 | tf_op jit(solution)/shard_map/while/body/eval_jaxpr/qhe,khe->hqk/dot_general | solution.py:89
  300.9 21.2 %multiply_convert_fusion.5 = bf16[12,512,1024]{2,1,0:T(8,128)(2,1)} fusion(f32[12,512,1024]{2,1,0:T(8,128)} %get-tuple-element.457, f32[12,512,1024]{2,1,0:T(8,128)} %fusion.125, f32[12,512]{1,0:T(8,128)S(1)} %get-tuple-element.458, f32[12,512]{1,0:T(8,128)S(1)} %dynamic-slice_bitcast_fusion.2, pred[512,1024]{1,0:T(8,128)(4,1)S(1)} %broadcast_compare_fusion.6), kind=kLoop, calls=%fused_computation.14.clone.1 | loop fusion | flops 37748736 | bytes 63488000 | tf_op jit(solution)/shard_map/while/body/eval_jaxpr/convert_element_type | solution.py:95
  322.2 9.7 %multiply_bitcast_fusion.3 = f32[1,512,12,64]{1,3,2,0:T(8,128)} fusion(bf16[12,512,1024]{2,1,0:T(8,128)(2,1)} %multiply_convert_fusion.5, bf16[1024,12,64]{0,2,1:T(8,128)(2,1)S(1)} %get-tuple-element.532), kind=kOutput, calls=%fused_computation.22.clone.1 | convolution fusion | flops 805699584 | bytes 15728640 | tf_op jit(solution)/shard_map/while/body/eval_jaxpr/hqk,khe->qhe/dot_general | solution.py:96
  334.9 28.8 %dynamic_update_slice.19 = f32[2,512,12,64]{1,0,3,2:T(2,128)} dynamic-update-slice(f32[2,512,12,64]{1,0,3,2:T(2,128)} %get-tuple-element.513, f32[1,512,12,64]{1,0,3,2:T(1,128)S(1)} %copy.132, s32[]{:T(128)} %get-tuple-element.510, s32[]{:T(128)} %constant.71.clone.1..sunk.1, s32[]{:T(128)} %constant.71.clone.1..sunk.1, s32[]{:T(128)} %constant.71.clone.1..sunk.1) | dynamic-update-slice | bytes 3145732 | tf_op jit(solution)/shard_map/while/body/jit(dynamic_update_index_in_dim)/dynamic_update_slice | solution.py:67
  363.7 8.9 %bitcast_add_fusion.4 = f32[1024,12,64]{0,2,1:T(8,128)} fusion(f32[1024,12,64]{0,2,1:T(8,128)} %get-tuple-element.511, bf16[12,512,1024]{2,1,0:T(8,128)(2,1)} %multiply_convert_fusion.5, pred[]{:T(512)S(6)} %compare.3, bf16[1024,12,64]{0,2,1:T(8,128)(2,1)} %copy-done.6, s32[]{:T(128)S(6)} %select_n.81), kind=kOutput, calls=%fused_computation.21.clone.1 | convolution fusion | flops 807665664 | bytes 19660804 | tf_op jit(solution)/shard_map/while/body/eval_jaxpr/hqk,qhe->khe/dot_general | solution.py:99
  372.6 13.4 %bitcast_add_fusion.5 = f32[1024,12,64]{0,2,1:T(8,128)} fusion(f32[1024,12,64]{0,2,1:T(8,128)} %get-tuple-element.512, f32[12,512,1024]{2,1,0:T(8,128)} %fusion.125, f32[12,512]{1,0:T(8,128)S(1)} %dynamic-slice_bitcast_fusion.2, pred[512,1024]{1,0:T(8,128)(4,1)S(1)} %copy-done.5, pred[]{:T(512)S(6)} %compare.3, ...), kind=kOutput, calls=%fused_computation.20.clone.1 | convolution fusion | flops 832045056 | bytes 32800772 | tf_op jit(solution)/shard_map/while/body/eval_jaxpr/hqk,qhe->khe/dot_general | solution.py:83
  387.3 10.1 %fusion.125 = f32[12,512,1024]{2,1,0:T(8,128)} fusion(bf16[1024,12,64]{0,2,1:T(8,128)(2,1)S(1)} %get-tuple-element.532, bf16[1024,12,64]{0,2,1:T(8,128)(2,1)S(1)} %get-tuple-element.530, s32[]{:T(128)S(6)} %select_n.81), kind=kOutput, calls=%fused_computation.28.clone.1 | convolution fusion | flops 805306368 | bytes 27525124 | tf_op jit(solution)/shard_map/while/body/eval_jaxpr/qhe,khe->hqk/dot_general | solution.py:44
  398.0 18.3 %multiply_reduce_fusion.11 = (f32[12,512]{1,0:T(8,128)S(1)}, f32[12,512,1024]{2,1,0:T(8,128)}) fusion(f32[12,512,1024]{2,1,0:T(8,128)} %fusion.125, f32[12,512]{1,0:T(8,128)S(1)} %dynamic-slice_bitcast_fusion.2, pred[512,1024]{1,0:T(8,128)(4,1)S(1)} %broadcast_compare_fusion.6, bf16[1024,12,64]{0,2,1:T(8,128)(2,1)} %get-tuple-element.535, ...), kind=kOutput, calls=%fused_computation.15.clone.1 | convolution fusion | flops 836757504 | bytes 53264388 | tf_op jit(solution)/shard_map/while/body/eval_jaxpr/qhe,khe->hqk/dot_general | solution.py:89
  416.2 21.2 %multiply_convert_fusion.5 = bf16[12,512,1024]{2,1,0:T(8,128)(2,1)} fusion(f32[12,512,1024]{2,1,0:T(8,128)} %get-tuple-element.457, f32[12,512,1024]{2,1,0:T(8,128)} %fusion.125, f32[12,512]{1,0:T(8,128)S(1)} %get-tuple-element.458, f32[12,512]{1,0:T(8,128)S(1)} %dynamic-slice_bitcast_fusion.2, pred[512,1024]{1,0:T(8,128)(4,1)S(1)} %broadcast_compare_fusion.6), kind=kLoop, calls=%fused_computation.14.clone.1 | loop fusion | flops 37748736 | bytes 63488000 | tf_op jit(solution)/shard_map/while/body/eval_jaxpr/convert_element_type | solution.py:95
  437.4 9.7 %multiply_bitcast_fusion.3 = f32[1,512,12,64]{1,3,2,0:T(8,128)} fusion(bf16[12,512,1024]{2,1,0:T(8,128)(2,1)} %multiply_convert_fusion.5, bf16[1024,12,64]{0,2,1:T(8,128)(2,1)S(1)} %get-tuple-element.532), kind=kOutput, calls=%fused_computation.22.clone.1 | convolution fusion | flops 805699584 | bytes 15728640 | tf_op jit(solution)/shard_map/while/body/eval_jaxpr/hqk,khe->qhe/dot_general | solution.py:96
  450.1 28.8 %dynamic_update_slice.19 = f32[2,512,12,64]{1,0,3,2:T(2,128)} dynamic-update-slice(f32[2,512,12,64]{1,0,3,2:T(2,128)} %get-tuple-element.513, f32[1,512,12,64]{1,0,3,2:T(1,128)S(1)} %copy.132, s32[]{:T(128)} %get-tuple-element.510, s32[]{:T(128)} %constant.71.clone.1..sunk.1, s32[]{:T(128)} %constant.71.clone.1..sunk.1, s32[]{:T(128)} %constant.71.clone.1..sunk.1) | dynamic-update-slice | bytes 3145732 | tf_op jit(solution)/shard_map/while/body/jit(dynamic_update_index_in_dim)/dynamic_update_slice | solution.py:67
  478.9 9.8 %bitcast_add_fusion.4 = f32[1024,12,64]{0,2,1:T(8,128)} fusion(f32[1024,12,64]{0,2,1:T(8,128)} %get-tuple-element.511, bf16[12,512,1024]{2,1,0:T(8,128)(2,1)} %multiply_convert_fusion.5, pred[]{:T(512)S(6)} %compare.3, bf16[1024,12,64]{0,2,1:T(8,128)(2,1)} %copy-done.6, s32[]{:T(128)S(6)} %select_n.81), kind=kOutput, calls=%fused_computation.21.clone.1 | convolution fusion | flops 807665664 | bytes 19660804 | tf_op jit(solution)/shard_map/while/body/eval_jaxpr/hqk,qhe->khe/dot_general | solution.py:99
  488.7 14.3 %bitcast_add_fusion.5 = f32[1024,12,64]{0,2,1:T(8,128)} fusion(f32[1024,12,64]{0,2,1:T(8,128)} %get-tuple-element.512, f32[12,512,1024]{2,1,0:T(8,128)} %fusion.125, f32[12,512]{1,0:T(8,128)S(1)} %dynamic-slice_bitcast_fusion.2, pred[512,1024]{1,0:T(8,128)(4,1)S(1)} %copy-done.5, pred[]{:T(512)S(6)} %compare.3, ...), kind=kOutput, calls=%fused_computation.20.clone.1 | convolution fusion | flops 832045056 | bytes 32800772 | tf_op jit(solution)/shard_map/while/body/eval_jaxpr/hqk,qhe->khe/dot_general | solution.py:83
  503.2 5.8 reshape.304
  512.0 4.5 convolution_convert_fusion.4
  516.7 10.2 %multiply_reduce_fusion.2 = (bf16[64]{0:T(256)(128)(2,1)S(1)}, f32[2,512,12]{1,0,2:T(2,128)S(1)}) fusion(f32[2,512,12,64]{1,0,3,2:T(2,128)S(1)} %copy-done.17, f32[2,512,12,64]{1,0,3,2:T(2,128)} %reshape.305, f32[2,512,12]{1,0,2:T(2,128)S(1)} %copy-done.50, f32[2,512,12]{1,0,2:T(2,128)S(1)} %get-tuple-element.321, f32[2,512,12]{1,0,2:T(2,128)S(1)} %get-tuple-element.320, ...), kind=kLoop, calls=%fused_computation.84 | loop fusion | flops 7851968 | bytes 6488448 | tf_op jit(solution)/shard_map/transpose(jvp())/reduce_sum | solution.py:18
  549.2 4.0 add_convert_fusion.2
  559.4 8.1 fusion.45
  568.7 5.9 convolution_convert_fusion.2
  575.4 9.9 %convolution_convert_fusion.1 = bf16[768,3072]{1,0:T(8,128)(2,1)} fusion(bf16[1024,3072]{1,0:T(8,128)(2,1)} %get-tuple-element.328, f32[1024,768]{0,1:T(8,128)} %copy-done.14, f32[768]{0:T(1024)S(1)} %copy-done.82, f32[768]{0:T(1024)S(1)} %copy-done.64, f32[1024]{0:T(1024)S(1)} %copy-done.66, f32[1024]{0:T(1024)S(1)} %copy-done.56), kind=kOutput, calls=%fused_computation.56 | convolution fusion | flops 4838129664 | bytes 14170112 | tf_op jit(solution)/shard_map/dot_general | solution.py:31
  587.1 9.8 %convolution_convert_fusion = bf16[3072,768]{1,0:T(8,128)(2,1)} fusion(bf16[1024,3072]{1,0:T(8,128)(2,1)} %get-tuple-element.309, bf16[1024,768]{0,1:T(8,128)(2,1)S(1)} %copy-done.21, pred[1024]{0:T(1024)(128)(4,1)S(1)} %copy-done.70), kind=kOutput, calls=%fused_computation.55 | convolution fusion | flops 4836556800 | bytes 12583936 | tf_op jit(solution)/shard_map/dot_general | solution.py:31
  600.1 9.0 %fusion.73 = (bf16[768]{0:T(1024)(128)(2,1)S(1)}, f32[1024,768]{1,0:T(8,128)}) fusion(bf16[768,2304]{1,0:T(8,128)(2,1)} %all-gather.6.cloned.1.call-done, bf16[1024,768]{1,0:T(8,128)(2,1)} %copy.96, bf16[1024,768]{1,0:T(8,128)(2,1)} %copy-done.24, bf16[1024,768]{1,0:T(8,128)(2,1)} %copy-done.28), kind=kOutput, calls=%fused_computation.140 | convolution fusion | flops 3638820096 | bytes 11404800 | tf_op jit(solution)/shard_map/dot_general | solution.py:37
  619.3 14.8 %all-reduce.21 = (bf16[768]{0:T(1024)(128)(2,1)S(1)}, bf16[2304]{0:T(1024)(128)(2,1)S(1)}, bf16[768]{0:T(1024)(128)(2,1)S(1)}, bf16[3072]{0:T(1024)(128)(2,1)S(1...) all-reduce(bf16[768]{0:T(1024)(128)(2,1)S(1)} %dynamic-update-slice, ...), channel_id=1, replica_groups=mesh['dp'=8,'fsdp'=4] {'fsdp'}, use_global_device_ids=true, to_apply=%add.8 | all-reduce | flops 10880 | bytes 43520
  634.8 13.9 %all-reduce.19 = (bf16[576]{0:T(1024)(128)(2,1)S(1)}, bf16[192]{0:T(256)(128)(2,1)S(1)}, bf16[768]{0:T(1024)(128)(2,1)S(1)}, bf16[192]{0:T(256)(128)(2,1)S(1)}, ...) all-reduce(bf16[576]{0:T(1024)(128)(2,1)S(1)} %dynamic-slice.10, ...), channel_id=1, replica_groups=mesh['dp'=8,'fsdp'=4] {'dp'}, use_global_device_ids=true, to_apply=%region_27.28 | all-reduce | flops 2528 | bytes 10112 | tf_op jit(solution)/shard_map/psum | solution.py:305
  654.3 5.6 add_convert_fusion.1
  662.7 24.3 %reduce-scatter.9.cloned.1.call-done = bf16[192,3072]{1,0:T(8,128)(2,1)} async-done(((bf16[768,3072]{1,0:T(8,128)(2,1)}), bf16[192,3072]{1,0:T(8,128)(2,1)}) %reduce-scatter.9.cloned.1.call-update) | async-done | bytes 1179664 | tf_op jit(solution)/shard_map/reduce_scatter | solution.py:272
  687.0 60.0 %reduce-scatter.11.cloned.1.call-done = bf16[768,768]{1,0:T(8,128)(2,1)} async-done(((bf16[3072,768]{1,0:T(8,128)(2,1)}), bf16[768,768]{1,0:T(8,128)(2,1)}) %reduce-scatter.11.cloned.1.call-update) | async-done | bytes 1179664 | tf_op jit(solution)/shard_map/reduce_scatter | solution.py:278
  747.0 9.5 %select_convert_fusion = bf16[1024,768]{0,1:T(8,128)(2,1)} fusion(f32[1024,768]{0,1:T(8,128)S(1)} %copy-done.16, bf16[1024,3072]{1,0:T(8,128)(2,1)} %get-tuple-element.309, bf16[3072,768]{1,0:T(8,128)(2,1)} %all-gather.12.cloned.1.call-done, f32[768]{0:T(1024)S(1)} %convert_element_type.215, pred[1024]{0:T(1024)(128)(4,1)S(1)} %copy-done.70), kind=kOutput, calls=%fused_computation.94 | convolution fusion | flops 4834983936 | bytes 15732736 | tf_op jit(solution)/shard_map/dot_general | solution.py:198
  759.1 74.7 %all-reduce.25.cloned.1.call-done = (bf16[192,2304]{1,0:T(8,128)(2,1)}, bf16[192,768]{1,0:T(8,128)(2,1)}, bf16[192,3072]{1,0:T(8,128)(2,1)}, bf16[768,768]{1,0:T(8,128)(2,1)}) async-done(((bf16[192,2304]{1,0:T(8,128)(2,1)}, bf16[192,768]{1,0:T(8,128)(2,1)}, bf16[192,3072]{1,0:T(8,128)(2,1)}, bf16[768,768]{1,0:T(8,128)(2,1)}), (bf16[192,2304]{1,0:T(8,128)(2,1)}, bf16[192,768]{1,0:T(8,128)(2,1)}, ...) | async-done | bytes 3538960 | tf_op jit(solution)/shard_map/psum | solution.py:304
  (378 shorter events, 142.5 us)
Async XLA Ops:
  7.3 7.2 copy-start.86
  7.3 26.5 %copy-start.35 = (bf16[1024,768]{1,0:T(8,128)(2,1)S(1)}, bf16[1024,768]{1,0:T(8,128)(2,1)}, u32[]{:S(2)}) copy-start(bf16[1024,768]{1,0:T(8,128)(2,1)} %param.21) | copy-start | bytes 4718596
  7.3 52.9 %all-gather.6.cloned.1.call-start = ((), (), s32[]{:S(2)}) async-start(), calls=%async_computation.4 | async-start | bytes 4423680 | tf_op jit(solution)/shard_map/all_gather | solution.py:131
  8.0 163.9 %all-gather.8.cloned.1.call-start = ((), (), s32[]{:S(2)}) async-start(), calls=%async_computation.5 | async-start | bytes 1474560 | tf_op jit(solution)/shard_map/all_gather | solution.py:133
  8.8 179.9 %all-gather.10.cloned.1.call-start = ((), (), s32[]{:S(2)}) async-start(), calls=%async_computation.6 | async-start | bytes 5898240 | tf_op jit(solution)/shard_map/all_gather | solution.py:135
  9.5 217.4 %all-gather.12.cloned.1.call-start = ((), (), s32[]{:S(2)}) async-start(), calls=%async_computation.7 | async-start | bytes 5898240 | tf_op jit(solution)/shard_map/all_gather | solution.py:137
  10.1 652.6 %reduce-scatter.7.cloned.1.call-start = ((), (), s32[]{:S(2)}) async-start(), calls=%async_computation.9 | async-start | bytes 1474560 | tf_op jit(solution)/shard_map/reduce_scatter | solution.py:266
  33.7 26.4 %copy-start.53 = (f32[768]{0:T(1024)}, f32[768]{0:T(1024)S(1)}, u32[]{:S(2)}) copy-start(f32[768]{0:T(1024)S(1)} %convert_element_type.198) | copy-start | bytes 9220
  33.7 26.4 %copy-start.79 = (f32[768]{0:T(1024)}, f32[768]{0:T(1024)S(1)}, u32[]{:S(2)}) copy-start(f32[768]{0:T(1024)S(1)} %convert_element_type.199) | copy-start | bytes 9220
  33.8 11.9 %copy-start.41 = (s32[1024]{0:T(1024)S(1)}, s32[1024]{0:T(1024)}, u32[]{:S(2)}) copy-start(s32[1024]{0:T(1024)} %param.22) | copy-start | bytes 12292
  34.5 25.6 %copy-start.11 = (bf16[1024,768]{0,1:T(8,128)(2,1)}, bf16[1024,768]{0,1:T(8,128)(2,1)S(1)}, u32[]{:S(2)}) copy-start(bf16[1024,768]{0,1:T(8,128)(2,1)S(1)} %copy.78) | copy-start | bytes 4718596
  34.6 11.6 %copy-start.36 = (bf16[1024,768]{1,0:T(8,128)(2,1)S(1)}, bf16[1024,768]{1,0:T(8,128)(2,1)}, u32[]{:S(2)}) copy-start(bf16[1024,768]{1,0:T(8,128)(2,1)} %param.23) | copy-start | bytes 4718596
  34.8 31.6 %copy-start.51 = (f32[1024]{0:T(1024)}, f32[1024]{0:T(1024)S(1)}, u32[]{:S(2)}) copy-start(f32[1024]{0:T(1024)S(1)} %broadcast_multiply_fusion.3) | copy-start | bytes 12292
  35.3 31.1 %copy-start.57 = (f32[1024]{0:T(1024)}, f32[1024]{0:T(1024)S(1)}, u32[]{:S(2)}) copy-start(f32[1024]{0:T(1024)S(1)} %fusion.54) | copy-start | bytes 12292
  35.4 53.1 %copy-start.77 = (f32[64]{0:T(128)}, f32[64]{0:T(128)S(1)}, u32[]{:S(2)}) copy-start(f32[64]{0:T(128)S(1)} %convert_element_type.202) | copy-start | bytes 772
  35.4 53.1 %copy-start.71 = (f32[64]{0:T(128)}, f32[64]{0:T(128)S(1)}, u32[]{:S(2)}) copy-start(f32[64]{0:T(128)S(1)} %convert_element_type.204) | copy-start | bytes 772
  76.1 12.4 %copy-start.32 = (f32[1024,12]{0,1:T(8,128)}, f32[1024,12]{0,1:T(8,128)S(1)}, u32[]{:S(2)}) copy-start(f32[1024,12]{0,1:T(8,128)S(1)} %broadcast_multiply_fusion.1) | copy-start | bytes 147460
  81.1 7.3 copy-start.43
  94.6 23.8 %copy-start.10 = (bf16[1024,12,64]{0,2,1:T(8,128)(2,1)S(1)}, bf16[1024,12,64]{0,2,1:T(8,128)(2,1)}, u32[]{:S(2)}) copy-start(bf16[1024,12,64]{0,2,1:T(8,128)(2,1)} %get-tuple-element.490) | copy-start | bytes 4718596 | tf_op jit(solution)/shard_map/while
  106.1 15.8 %copy-start = (f32[12,512,1024]{2,1,0:T(8,128)S(1)}, f32[12,512,1024]{2,1,0:T(8,128)}, u32[]{:S(2)}) copy-start(f32[12,512,1024]{2,1,0:T(8,128)} %get-tuple-element.444) | copy-start | bytes 75497472 | tf_op jit(solution)/shard_map/while
  132.1 23.0 %copy-start.10 = (bf16[1024,12,64]{0,2,1:T(8,128)(2,1)S(1)}, bf16[1024,12,64]{0,2,1:T(8,128)(2,1)}, u32[]{:S(2)}) copy-start(bf16[1024,12,64]{0,2,1:T(8,128)(2,1)} %get-tuple-element.490) | copy-start | bytes 4718596 | tf_op jit(solution)/shard_map/while
  142.7 16.1 %copy-start = (f32[12,512,1024]{2,1,0:T(8,128)S(1)}, f32[12,512,1024]{2,1,0:T(8,128)}, u32[]{:S(2)}) copy-start(f32[12,512,1024]{2,1,0:T(8,128)} %get-tuple-element.444) | copy-start | bytes 75497472 | tf_op jit(solution)/shard_map/while
  175.8 88.6 %copy-start.55 = (f32[1024]{0:T(1024)}, f32[1024]{0:T(1024)S(1)}, u32[]{:S(2)}) copy-start(f32[1024]{0:T(1024)S(1)} %broadcast_multiply_fusion.2) | copy-start | bytes 12292
  176.7 87.7 %copy-start.65 = (f32[1024]{0:T(1024)}, f32[1024]{0:T(1024)S(1)}, u32[]{:S(2)}) copy-start(f32[1024]{0:T(1024)S(1)} %fusion.55) | copy-start | bytes 12292
  188.7 38.2 %copy-start.69 = (pred[1024]{0:T(1024)(128)(4,1)S(1)}, pred[1024]{0:T(1024)(128)(4,1)}, u32[]{:S(2)}) copy-start(pred[1024]{0:T(1024)(128)(4,1)} %broadcast_compare_fusion.2) | copy-start | bytes 3076
  270.7 11.5 %copy-start.6 = (bf16[1024,12,64]{0,2,1:T(8,128)(2,1)}, bf16[1024,12,64]{0,2,1:T(8,128)(2,1)S(1)}, u32[]{:S(2)}) copy-start(bf16[1024,12,64]{0,2,1:T(8,128)(2,1)S(1)} %get-tuple-element.530) | copy-start | bytes 4718596 | tf_op jit(solution)/shard_map/while
  282.7 18.3 %copy-start.4 = (pred[512,1024]{1,0:T(8,128)(4,1)}, pred[512,1024]{1,0:T(8,128)(4,1)S(1)}, u32[]{:S(2)}) copy-start(pred[512,1024]{1,0:T(8,128)(4,1)S(1)} %broadcast_compare_fusion.6) | copy-start | bytes 1572868 | tf_op jit(solution)/shard_map/while
  363.7 8.9 %copy-start.5 = (pred[512,1024]{1,0:T(8,128)(4,1)S(1)}, pred[512,1024]{1,0:T(8,128)(4,1)}, u32[]{:S(2)}) copy-start(pred[512,1024]{1,0:T(8,128)(4,1)} %copy-done.4) | copy-start | bytes 1572868 | tf_op jit(solution)/shard_map/while
  363.7 8.9 %copy-start.23 = (bf16[1024,12,64]{0,2,1:T(8,128)(2,1)S(1)}, bf16[1024,12,64]{0,2,1:T(8,128)(2,1)}, u32[]{:S(2)}) copy-start(bf16[1024,12,64]{0,2,1:T(8,128)(2,1)} %get-tuple-element.534) | copy-start | bytes 4718596 | tf_op jit(solution)/shard_map/while
  372.6 13.4 %copy-start.7 = (bf16[1024,12,64]{0,2,1:T(8,128)(2,1)S(1)}, bf16[1024,12,64]{0,2,1:T(8,128)(2,1)}, u32[]{:S(2)}) copy-start(bf16[1024,12,64]{0,2,1:T(8,128)(2,1)} %copy-done.6) | copy-start | bytes 4718596 | tf_op jit(solution)/shard_map/while
  386.0 11.5 %copy-start.6 = (bf16[1024,12,64]{0,2,1:T(8,128)(2,1)}, bf16[1024,12,64]{0,2,1:T(8,128)(2,1)S(1)}, u32[]{:S(2)}) copy-start(bf16[1024,12,64]{0,2,1:T(8,128)(2,1)S(1)} %get-tuple-element.530) | copy-start | bytes 4718596 | tf_op jit(solution)/shard_map/while
  397.9 18.3 %copy-start.4 = (pred[512,1024]{1,0:T(8,128)(4,1)}, pred[512,1024]{1,0:T(8,128)(4,1)S(1)}, u32[]{:S(2)}) copy-start(pred[512,1024]{1,0:T(8,128)(4,1)S(1)} %broadcast_compare_fusion.6) | copy-start | bytes 1572868 | tf_op jit(solution)/shard_map/while
  478.9 9.8 %copy-start.5 = (pred[512,1024]{1,0:T(8,128)(4,1)S(1)}, pred[512,1024]{1,0:T(8,128)(4,1)}, u32[]{:S(2)}) copy-start(pred[512,1024]{1,0:T(8,128)(4,1)} %copy-done.4) | copy-start | bytes 1572868 | tf_op jit(solution)/shard_map/while
  478.9 9.8 %copy-start.23 = (bf16[1024,12,64]{0,2,1:T(8,128)(2,1)S(1)}, bf16[1024,12,64]{0,2,1:T(8,128)(2,1)}, u32[]{:S(2)}) copy-start(bf16[1024,12,64]{0,2,1:T(8,128)(2,1)} %get-tuple-element.534) | copy-start | bytes 4718596 | tf_op jit(solution)/shard_map/while
  488.7 14.3 %copy-start.7 = (bf16[1024,12,64]{0,2,1:T(8,128)(2,1)S(1)}, bf16[1024,12,64]{0,2,1:T(8,128)(2,1)}, u32[]{:S(2)}) copy-start(bf16[1024,12,64]{0,2,1:T(8,128)(2,1)} %copy-done.6) | copy-start | bytes 4718596 | tf_op jit(solution)/shard_map/while
  548.9 113.8 %reduce-scatter.5.cloned.1.call-start = ((), (), s32[]{:S(2)}) async-start(), calls=%async_computation.8 | async-start | bytes 4423680 | tf_op jit(solution)/shard_map/reduce_scatter | solution.py:260
  555.1 12.4 %copy-start.24 = (bf16[1024,768]{1,0:T(8,128)(2,1)}, bf16[1024,768]{1,0:T(8,128)(2,1)S(1)}, u32[]{:S(2)}) copy-start(bf16[1024,768]{1,0:T(8,128)(2,1)S(1)} %copy.95) | copy-start | bytes 4718596
  559.4 9.3 %copy-start.12 = (bf16[1024,768]{0,1:T(8,128)(2,1)S(1)}, bf16[1024,768]{0,1:T(8,128)(2,1)}, u32[]{:S(2)}) copy-start(bf16[1024,768]{0,1:T(8,128)(2,1)} %copy-done.11) | copy-start | bytes 4718596
  559.4 9.3 %copy-start.26 = (bf16[1024,768]{1,0:T(8,128)(2,1)S(1)}, bf16[1024,768]{1,0:T(8,128)(2,1)}, u32[]{:S(2)}) copy-start(bf16[1024,768]{1,0:T(8,128)(2,1)} %copy.96) | copy-start | bytes 4718596
  559.4 9.3 %copy-start.52 = (f32[1024]{0:T(1024)S(1)}, f32[1024]{0:T(1024)}, u32[]{:S(2)}) copy-start(f32[1024]{0:T(1024)} %copy-done.51) | copy-start | bytes 12292
  559.4 9.3 %copy-start.54 = (f32[768]{0:T(1024)S(1)}, f32[768]{0:T(1024)}, u32[]{:S(2)}) copy-start(f32[768]{0:T(1024)} %copy-done.53) | copy-start | bytes 9220
  559.4 9.3 %copy-start.58 = (f32[1024]{0:T(1024)S(1)}, f32[1024]{0:T(1024)}, u32[]{:S(2)}) copy-start(f32[1024]{0:T(1024)} %copy-done.57) | copy-start | bytes 12292
  559.4 9.3 %copy-start.80 = (f32[768]{0:T(1024)S(1)}, f32[768]{0:T(1024)}, u32[]{:S(2)}) copy-start(f32[768]{0:T(1024)} %copy-done.79) | copy-start | bytes 9220
  574.7 112.4 %reduce-scatter.9.cloned.1.call-start = ((), (), s32[]{:S(2)}) async-start(), calls=%async_computation.10 | async-start | bytes 5898240 | tf_op jit(solution)/shard_map/reduce_scatter | solution.py:272
  585.3 161.8 %reduce-scatter.11.cloned.1.call-start = ((), (), s32[]{:S(2)}) async-start(), calls=%async_computation.11 | async-start | bytes 5898240 | tf_op jit(solution)/shard_map/reduce_scatter | solution.py:278
  596.9 237.0 %all-reduce.25.cloned.1.call-start = ((), (), s32[]{:S(2)}) async-start(), calls=%async_computation.12 | async-start | bytes 7077888 | tf_op jit(solution)/shard_map/psum | solution.py:304
  617.9 36.4 %copy-start.60 = (f32[1024]{0:T(1024)S(1)}, f32[1024]{0:T(1024)}, u32[]{:S(2)}) copy-start(f32[1024]{0:T(1024)} %copy-done.59) | copy-start | bytes 12292
  660.0 87.1 %copy-start.16 = (f32[1024,768]{0,1:T(8,128)S(1)}, f32[1024,768]{0,1:T(8,128)}, u32[]{:S(2)}) copy-start(f32[1024,768]{0,1:T(8,128)} %copy-done.14) | copy-start | bytes 9437188
  (65 other events, 218.1 us)
Sparse Core Ops, SparseCore 0:
  9.9 50.1 all-gather.5
  62.0 27.5 all-gather.7
  91.4 56.9 all-gather.9
  150.1 56.9 all-gather.11
  549.1 27.3 reduce-scatter.6
  579.4 47.5 reduce-scatter.4
  630.0 57.0 reduce-scatter.8
  690.0 56.9 reduce-scatter.10
  749.7 84.1 all-reduce.24
where the time goes:
time: 856 us; the launch traced here: 848 us
  matrix products  291 us (34%)
  waiting for transfers between devices  173 us (20%)
  local copies, waits for them, and re-layouts  162 us (19%)
  other arithmetic  141 us (16%)
  blocking collectives  55.5 us (6%)
  between operations  20 us (2%)
    psum x1, waiting for transfers between devices, shards(): lax.psum(summed[0].astype(jnp.bfloat16), 'dp').astype(jnp.float32)  74.7 us
    dynamic_update_slice x4, local copies, waits for them, and re-layouts, attend(): lax.map(one_block, jnp.arange(count // block, dtype=jnp.int32))  63.6 us
    reduce_scatter x1, waiting for transfers between devices, shards(): lax.psum_scatter(down_grad.astype(jnp.bfloat16), 'fsdp', scatter_dimensio...  60 us
    convert_element_type x2, other arithmetic, one_block(): scores_low = grad_scores.astype(jnp.bfloat16)  42.4 us
    dot_general x4, matrix products, block_scores(): jnp.einsum('qhe,khe->hqk', query_block, key_low, preferred_element_type=j...  42.4 us
    dot_general x4, matrix products, right_product(): lax.dot_general(left, right, (((1,), (1,)), ((), ())), preferred_element_...  41.1 us
    dot_general x1, matrix products, shards(): jnp.dot(second_low, up_matrix, preferred_element_type=jnp.float32)  38.1 us
    dot_general x2, matrix products, one_block(): jnp.einsum('qhe,khe->hqk', grad_block, value_low, preferred_element_type=...  36.5 us
  transfers between devices with their start and end apart: 9, of which 4 were waited for; matrix products, arithmetic and copies ran while one was open for 30% of the time, Pallas kernels for 0%

commit v1 on v0

v1 whole, which is shorter than its diff:
```python
import functools

import jax
import jax.numpy as jnp
from jax import lax
from jax.experimental import pallas as pl
from jax.experimental.pallas import tpu as pltpu
from jax.sharding import PartitionSpec as P

norm_eps = 1e-06
low = jnp.bfloat16
full = jnp.float32


def layer_norm(value, gain, shift):
    centred = value - jnp.mean(value, axis=-1, keepdims=True)
    scaled = centred * lax.rsqrt(jnp.mean(centred * centred, axis=-1, keepdims=True) + norm_eps)
    return scaled * gain + shift


def exact_gelu(value):
    return jax.nn.gelu(value, approximate=False)


def left_product(left, right):
    return lax.dot_general(
        left, right, (((0,), (0,)), ((), ())), preferred_element_type=jnp.float32
    )


def right_product(left, right):
    return lax.dot_general(
        left, right, (((1,), (1,)), ((), ())), preferred_element_type=jnp.float32
    )


def plain(left, right):
    return jnp.dot(left, right, preferred_element_type=jnp.float32)


def lane_index(shape):
    return lax.broadcasted_iota(jnp.int32, shape, len(shape) - 1)


def same_head(scale):
    row = lax.broadcasted_iota(jnp.int32, (128, 128), 0) // 64
    column = lax.broadcasted_iota(jnp.int32, (128, 128), 1) // 64
    return jnp.where(row == column, scale, 0.0).astype(low)


def head_norm(raw, mean_map):
    value = raw.astype(full)
    centred = value - plain(raw, mean_map)
    scale = lax.rsqrt(plain((centred * centred).astype(low), mean_map) + norm_eps)
    return centred * scale, scale


def half_mask(head, lanes):
    return (lanes < 64) if head == 0 else (lanes >= 64)


def query_codes(segments, lanes):
    spot = lanes % 64
    match = jnp.where(spot == segments + 1, 128.0, 0.0)
    return jnp.where(spot == 17, -128.0, match)


def key_codes(segments, lanes):
    spot = lanes % 64
    match = jnp.where(spot == segments + 1, 1.0, 0.0)
    return jnp.where((spot >= 17) & (spot < 20), 1.0, match)


def spans(count):
    cut = count * 9 // 16
    return ((0, cut), (cut, count))


def attend_kernel(flag_ref, q_ref, k_ref, v_ref, seg_ref, gq_ref, gk_ref, o_ref, total_ref):
    count = q_ref.shape[0]
    lanes = lane_index((count, 128))
    mean_map = same_head(1.0 / 64)
    q_unit, _ = head_norm(q_ref[...], mean_map)
    k_unit, _ = head_norm(k_ref[...], mean_map)
    q_low = q_unit * (gq_ref[...] * 0.125)
    k_low = k_unit * gk_ref[...]
    segments = seg_ref[...]
    q_code = query_codes(segments, lanes)
    k_code = key_codes(segments, lanes)
    values = v_ref[...]
    q_heads = [jnp.where(half_mask(h, lanes), q_low, q_code).astype(low) for h in (0, 1)]
    k_heads = [jnp.where(half_mask(h, lanes), k_low, k_code).astype(low) for h in (0, 1)]
    v_heads = [
        jnp.where(half_mask(h, lanes), values.astype(full), 1.0).astype(low) for h in (0, 1)
    ]

    def run(first, last, keys_first, keys_last, tile):
        for start in range(first, last, tile):
            parts = []
            for h in (0, 1):
                scores = right_product(
                    q_heads[h][start : start + tile], k_heads[h][keys_first:keys_last]
                )
                parts.append(plain(jnp.exp(scores).astype(low), v_heads[h][keys_first:keys_last]))
            here = lane_index((tile, 128)) < 64
            raw = jnp.where(here, parts[0], parts[1])
            sums = jnp.where(here, parts[1], parts[0])
            total = pltpu.roll(sums, 64, 1)
            o_ref[start : start + tile] = (raw / total).astype(o_ref.dtype)
            total_ref[start : start + tile] = jnp.log(sums)

    @pl.when(flag_ref[0] == 0)
    def _():
        for first, last in spans(count):
            run(first, last, first, last, (last - first) // 2)

    @pl.when(flag_ref[0] != 0)
    def _():
        run(0, count, 0, count, 256)


def attend_back_kernel(
    flag_ref,
    q_ref,
    k_ref,
    v_ref,
    seg_ref,
    gq_ref,
    gk_ref,
    o_ref,
    total_ref,
    do_ref,
    grad_ref,
    gain_ref,
    dq_scr,
):
    count = q_ref.shape[0]
    lanes = lane_index((count, 128))
    spot = lanes % 64
    mean_map = same_head(1.0 / 64)
    q_unit, q_scale = head_norm(q_ref[...], mean_map)
    k_unit, k_scale = head_norm(k_ref[...], mean_map)
    q_low = (q_unit * (gq_ref[...] * 0.125)).astype(low)
    k_low = (k_unit * gk_ref[...]).astype(low)
    segments = seg_ref[...]
    log_total = total_ref[...]
    log_high = log_total.astype(low).astype(full)
    q_code = jnp.where(
        spot == 18,
        -log_high,
        jnp.where(spot == 19, log_high - log_total, query_codes(segments, lanes)),
    ).astype(low)
    k_code = key_codes(segments, lanes).astype(low)
    grads = do_ref[...]
    product = (grads.astype(full) * o_ref[...].astype(full)).astype(low)
    row = lax.broadcasted_iota(jnp.int32, (128, 128), 0) // 64
    column = lax.broadcasted_iota(jnp.int32, (128, 128), 1) // 64
    delta = plain(product, jnp.where(row != column, 1.0, 0.0).astype(low))
    delta_high = delta.astype(low).astype(full)
    g_code = jnp.where(
        spot == 0, -delta_high, jnp.where(spot == 1, delta_high - delta, 0.0)
    ).astype(low)
    v_code = jnp.where(spot < 2, 1.0, 0.0).astype(low)
    values = v_ref[...]
    masks = [half_mask(h, lanes) for h in (0, 1)]
    q_heads = [jnp.where(masks[h], q_low, q_code) for h in (0, 1)]
    k_heads = [jnp.where(masks[h], k_low, k_code) for h in (0, 1)]
    v_heads = [jnp.where(masks[h], values, v_code) for h in (0, 1)]
    g_heads = [jnp.where(masks[h], grads, g_code) for h in (0, 1)]
    dk_parts = []

    def run(first, last, other_first, other_last, tile):
        for start in range(first, last, tile):
            rows = slice(start, start + tile)
            others = slice(other_first, other_last)
            dv_parts, dk_parts, dq_parts = [], [], []
            for h in (0, 1):
                scores = right_product(k_heads[h][rows], q_heads[h][others])
                weights = jnp.exp(scores)
                change = right_product(v_heads[h][rows], g_heads[h][others])
                sloped = (weights * change).astype(low)
                dv_parts.append(plain(weights.astype(low), grads[others]))
                dk_parts.append(plain(sloped, q_low[others]))
                dq_parts.append(left_product(sloped, k_low[rows]))
            here = lane_index((tile, 128)) < 64
            there = lane_index((other_last - other_first, 128)) < 64
            grad_ref[2, rows] = jnp.where(here, dv_parts[0], dv_parts[1]).astype(low)
            dk = jnp.where(here, dk_parts[0], dk_parts[1])
            dk_scr_store(rows, dk)
            dq = jnp.where(there, dq_parts[0], dq_parts[1])
            if start == first:
                dq_scr[0, others] = dq
            else:
                dq_scr[0, others] += dq

    def dk_scr_store(rows, value):
        dq_scr[1, rows] = value

    @pl.when(flag_ref[0] == 0)
    def _():
        for first, last in spans(count):
            run(first, last, first, last, (last - first) // 2)

    @pl.when(flag_ref[0] != 0)
    def _():
        run(0, count, 0, count, 256)

    def norm_back(slot, factor, unit, scale, gain):
        slope = dq_scr[slot] * factor
        inner = slope * gain
        shared = inner * unit
        result = scale * (
            inner
            - plain(inner.astype(low), mean_map)
            - unit * plain(shared.astype(low), mean_map)
        )
        grad_ref[slot] = result.astype(low)
        gain_ref[0, slot : slot + 1] = jnp.sum(slope * unit, axis=0, keepdims=True)

    norm_back(0, 0.125, q_unit, q_scale, gq_ref[...])
    norm_back(1, 1.0, k_unit, k_scale, gk_ref[...])


def attend_specs(count, width):
    pairs = width // 128
    column = lambda offset: pl.BlockSpec((count, 128), lambda i, flag: (0, i + offset))
    fixed = lambda shape: pl.BlockSpec(shape, lambda i, flag: (0, 0))
    shared = [
        column(0),
        column(pairs),
        column(2 * pairs),
        fixed((count, 1)),
        fixed((1, 128)),
        fixed((1, 128)),
    ]
    return pairs, column, shared


def attend(flag, mixed, segments, gain_q, gain_k):
    count = mixed.shape[0]
    width = mixed.shape[1] // 3
    pairs, column, shared = attend_specs(count, width)
    return pl.pallas_call(
        attend_kernel,
        grid_spec=pltpu.PrefetchScalarGridSpec(
            num_scalar_prefetch=1,
            grid=(pairs,),
            in_specs=shared,
            out_specs=[column(0), column(0)],
        ),
        out_shape=[
            jax.ShapeDtypeStruct((count, width), low),
            jax.ShapeDtypeStruct((count, width), full),
        ],
        compiler_params=pltpu.CompilerParams(vmem_limit_bytes=50 * 2**20),
        cost_estimate=pl.CostEstimate(
            flops=16 * count * count * width,
            bytes_accessed=count * width * 12,
            transcendentals=count * count * width // 64,
        ),
        name="attend",
    )(flag, mixed, mixed, mixed, segments, gain_q, gain_k)


def attend_back(flag, mixed, segments, gain_q, gain_k, attended, log_total, grad):
    count = mixed.shape[0]
    width = mixed.shape[1] // 3
    pairs, column, shared = attend_specs(count, width)
    return pl.pallas_call(
        attend_back_kernel,
        grid_spec=pltpu.PrefetchScalarGridSpec(
            num_scalar_prefetch=1,
            grid=(pairs,),
            in_specs=shared + [column(0), column(0), column(0)],
            out_specs=[
                pl.BlockSpec((3, count, 128), lambda i, flag: (0, 0, i)),
                pl.BlockSpec((1, 2, 128), lambda i, flag: (i, 0, 0)),
            ],
            scratch_shapes=[pltpu.VMEM((2, count, 128), full)],
        ),
        out_shape=[
            jax.ShapeDtypeStruct((3, count, width), low),
            jax.ShapeDtypeStruct((pairs, 2, 128), full),
        ],
        compiler_params=pltpu.CompilerParams(vmem_limit_bytes=56 * 2**20),
        cost_estimate=pl.CostEstimate(
            flops=40 * count * count * width,
            bytes_accessed=count * width * 18,
            transcendentals=count * count * width // 64,
        ),
        name="attend_back",
    )(flag, mixed, mixed, mixed, segments, gain_q, gain_k, attended, log_total, grad)


def gather_small(parts):
    lengths = [part.shape[0] for part in parts]
    flat = jnp.concatenate(parts).reshape(1, -1)
    whole = lax.all_gather(flat, "fsdp", axis=0, tiled=True)
    result, start = [], 0
    for length in lengths:
        result.append(whole[:, start : start + length].reshape(-1))
        start += length
    return result


def sum_small(parts, groups):
    lengths = [part.shape[0] // groups for part in parts]
    rows = jnp.concatenate([part.reshape(groups, -1) for part in parts], axis=1).astype(low)
    mine = lax.psum_scatter(rows, "fsdp", scatter_dimension=0, tiled=True)
    mine = lax.psum(mine, "dp").astype(full).reshape(-1)
    result, start = [], 0
    for length in lengths:
        result.append(mine[start : start + length])
        start += length
    return result


def sum_large(part):
    mine = lax.psum_scatter(part.astype(low), "fsdp", scatter_dimension=0, tiled=True)
    return lax.psum(mine, "dp").astype(full)


def gather_large(part):
    return lax.all_gather(part, "fsdp", axis=0, tiled=True)


def shards(
    groups,
    tokens,
    segments,
    cotangent,
    qkv_weight,
    qkv_bias,
    out_weight,
    out_bias,
    up_weight,
    up_bias,
    down_weight,
    down_bias,
    first_gain,
    first_shift,
    second_gain,
    second_shift,
    query_gain,
    key_gain,
):
    small = gather_small(
        [
            qkv_bias,
            out_bias,
            up_bias,
            down_bias,
            first_gain,
            first_shift,
            second_gain,
            second_shift,
            query_gain,
            key_gain,
        ]
    )
    small = [part.astype(full) for part in small]
    (qkv_b, out_b, up_b, down_b, gain_1, shift_1, gain_2, shift_2, gain_q, gain_k) = small
    qkv_w = gather_large(qkv_weight)
    out_w = gather_large(out_weight)
    up_w = gather_large(up_weight)
    down_w = gather_large(down_weight)
    count, width = tokens.shape
    cut = spans(count)[0][1]
    crossing = jnp.any(segments[:cut, None] == segments[None, cut:])
    flag = crossing.astype(jnp.int32).reshape(1)
    column = segments.reshape(count, 1)
    pair_q = jnp.tile(gain_q, 2).reshape(1, 128)
    pair_k = jnp.tile(gain_k, 2).reshape(1, 128)
    valid = (segments >= 0)[:, None]

    inputs = tokens.astype(full)
    normed, first_back = jax.vjp(layer_norm, inputs, gain_1, shift_1)
    normed = normed.astype(low)
    mixed = (plain(normed, qkv_w) + qkv_b).astype(low)
    attended, log_total = attend(flag, mixed, column, pair_q, pair_k)
    residual = inputs + plain(attended, out_w) + out_b
    second, second_back = jax.vjp(layer_norm, residual, gain_2, shift_2)
    second = second.astype(low)
    hidden = plain(second, up_w) + up_b
    active, gelu_back = jax.vjp(exact_gelu, hidden)
    active = active.astype(low)
    output = jnp.where(valid, residual + plain(active, down_w) + down_b, 0.0).astype(low)

    grad_low = jnp.where(valid, cotangent, jnp.zeros_like(cotangent))
    grad_output = grad_low.astype(full)
    down_grad = sum_large(left_product(active, grad_low))
    down_b_grad = jnp.sum(grad_output, axis=0)
    (grad_hidden,) = gelu_back(right_product(grad_low, down_w))
    grad_hidden = grad_hidden.astype(low)
    up_grad = sum_large(left_product(second, grad_hidden))
    up_b_grad = jnp.sum(grad_hidden.astype(full), axis=0)
    grad_norm_2, gain_2_grad, shift_2_grad = second_back(right_product(grad_hidden, up_w))
    grad_residual = grad_output + grad_norm_2
    branch = grad_residual.astype(low)
    out_grad = sum_large(left_product(attended, branch))
    out_b_grad = jnp.sum(branch.astype(full), axis=0)
    grad_attended = right_product(branch, out_w).astype(low)
    grad_mixed, pair_gains = attend_back(
        flag, mixed, column, pair_q, pair_k, attended, log_total, grad_attended
    )
    gain_sums = jnp.sum(pair_gains, axis=0).reshape(2, 2, -1).sum(axis=1)
    pieces = [grad_mixed[i] for i in range(3)]
    qkv_grad = sum_large(
        jnp.concatenate([left_product(normed, piece).astype(low) for piece in pieces], axis=1)
    )
    qkv_b_grad = jnp.sum(grad_mixed.astype(full), axis=1).reshape(-1)
    grad_norm = sum(
        right_product(piece, qkv_w[:, i * width : (i + 1) * width])
        for i, piece in enumerate(pieces)
    )
    grad_norm_1, gain_1_grad, shift_1_grad = first_back(grad_norm)
    grad_input = (grad_residual + grad_norm_1).astype(low)
    sums = sum_small(
        [
            qkv_b_grad,
            out_b_grad,
            up_b_grad,
            down_b_grad,
            gain_1_grad,
            shift_1_grad,
            gain_2_grad,
            shift_2_grad,
            gain_sums[0],
            gain_sums[1],
        ],
        groups,
    )
    return (
        output,
        grad_input,
        qkv_grad,
        sums[0],
        out_grad,
        sums[1],
        up_grad,
        sums[2],
        down_grad,
        sums[3],
        *sums[4:],
    )


def solution(mesh):
    rows = P(("dp", "fsdp"), None)
    matrix = P("fsdp", None)
    vector = P("fsdp")
    params = (matrix, vector) * 4 + (vector,) * 6
    return jax.shard_map(
        functools.partial(shards, mesh.shape["fsdp"]),
        mesh=mesh,
        in_specs=(rows, P(("dp", "fsdp")), rows) + params,
        out_specs=(rows, rows) + params,
        check_vma=False,
    )
```

time: 856 us -> 613 us (0.72)
  matrix products: 291 us -> 130 us
  local copies, waits for them, and re-layouts: 162 us -> 35.4 us
  other arithmetic: 141 us -> 25.3 us
  waiting for transfers between devices: 173 us -> 282 us
  Pallas kernels: 0 us -> 53.6 us
    dot_general x18 -> x4, matrix products: 220 us -> 58.6 us  [plain(): return jnp.dot(left, right, preferred_element_type=jnp.float32)]
    all_gather x4, waiting for transfers between devices: 11.7 us -> 96.9 us  [gather_large(): return lax.all_gather(part, 'fsdp', axis=0, tiled=True)]
    dynamic_update_slice x4 -> x0, local copies, waits for them, and re-layouts: 63.6 us -> none  [attend(): lax.map(one_block, jnp.arange(count // block, dtype=jnp.int32))]
    reduce_scatter x4 -> x3, waiting for transfers between devices: 84.3 us -> 142 us  [sum_large(): lax.psum_scatter(part.astype(low), 'fsdp', scatter_dimension=0, tiled=True)]
    convert_element_type x28 -> x9, other arithmetic: 67.1 us -> 10.3 us  [the longest x1 5.54 us: shards(): grad_input = (grad_residual + grad_norm_1).astype(low)]
    pallas_call x0 -> x2, Pallas kernels: none -> 53.6 us  [the longest x1 34.4 us: attend_back(): pl.pallas_call(attend_back_kernel, grid_spec=pltpu.PrefetchScalarGridSpec...]
    reduce_sum x13 -> x4, other arithmetic: 49.3 us -> 3.95 us  [the longest x1 3.12 us: shards(): qkv_b_grad = jnp.sum(grad_mixed.astype(full), axis=1).reshape(-1)]
    psum x1, waiting for transfers between devices: 74.7 us -> 40.1 us  [sum_large(): return lax.psum(mine, 'dp').astype(full)]
  transfers between devices with their start and end apart: 9 -> 9, of which waited for: 4 -> 8; matrix products, arithmetic and copies ran while one was open for 30% -> 21% of each run, Pallas kernels for 0% -> 3%
where the time goes in v1:
time: 613 us; the launch traced here: 603 us
  waiting for transfers between devices  282 us (46%)
  matrix products  130 us (21%)
  blocking collectives  60.9 us (10%)
  Pallas kernels  53.6 us (9%)
  local copies, waits for them, and re-layouts  35.4 us (6%)
  other arithmetic  25.3 us (4%)
  between operations  16.2 us (3%)
    reduce_scatter x3, waiting for transfers between devices, sum_large(): lax.psum_scatter(part.astype(low), 'fsdp', scatter_dimension=0, tiled=True)  142 us
    all_gather x4, waiting for transfers between devices, gather_large(): return lax.all_gather(part, 'fsdp', axis=0, tiled=True)  96.9 us
    dot_general x4, matrix products, plain(): return jnp.dot(left, right, preferred_element_type=jnp.float32)  58.6 us
    dot_general x6, matrix products, right_product(): lax.dot_general(left, right, (((1,), (1,)), ((), ())), preferred_element_...  40.7 us
    psum x1, waiting for transfers between devices, sum_large(): return lax.psum(mine, 'dp').astype(full)  40.1 us
    pallas_call x1, Pallas kernels, attend_back(): pl.pallas_call(attend_back_kernel, grid_spec=pltpu.PrefetchScalarGridSpec...  34.4 us
    unnamed x2, blocking collectives  33.7 us
    dot_general x6, matrix products, left_product(): lax.dot_general(left, right, (((0,), (0,)), ((), ())), preferred_element_...  30.4 us
  transfers between devices with their start and end apart: 9, of which 8 were waited for; matrix products, arithmetic and copies ran while one was open for 21% of the time, Pallas kernels for 3%

profile of v1, /device:TPU:0, one launch (start us, length us, event | category | flops | bytes accessed | tf_op | source)
XLA Modules:
  0.0 603.1 jit_solution(2503589416848579547)
XLA Ops:
  12.0 18.4 %all-reduce = bf16[10112]{0:T(1024)(128)(2,1)S(1)} all-reduce(bf16[10112]{0:T(1024)(128)(2,1)S(1)} %dynamic-update-slice), channel_id=2, replica_groups=mesh['dp'=8,'fsdp'=4] {'fsdp'}, use_global_device_ids=true, to_apply=%add | all-reduce | flops 10112 | bytes 40448
  33.7 1.9 copy.70
  37.0 2.6 copy.73
  39.6 20.5 %all-gather.6.cloned.1.call-done = bf16[768,2304]{1,0:T(8,128)(2,1)} async-done(((bf16[192,2304]{1,0:T(8,128)(2,1)}), bf16[768,2304]{1,0:T(8,128)(2,1)}) %all-gather.6.cloned.1.call-update) | async-done | bytes 3538960 | tf_op jit(solution)/shard_map/all_gather | solution.py:324
  60.1 7.9 %add_convert_fusion.1.q_ref.k_ref.v_ref = bf16[1024,2304]{1,0:T(8,128)(2,1)} fusion(bf16[768,2304]{1,0:T(8,128)(2,1)} %all-gather.6.cloned.1.call-done, f32[2304]{0:T(1024)S(1)} %reshape.248, bf16[1024,768]{0,1:T(8,128)(2,1)S(1)} %copy.70, f32[768]{0:T(1024)S(1)} %reshape.247, f32[768]{0:T(1024)S(1)} %reshape.246, f32[1024]{0:T(1024)S(1)} %fusion.52, ...), kind=kOutput, calls=%fused_computation.17 | convolution fusion | flops 3633315840 | bytes 9853952 | tf_op jit(solution)/shard_map/dot_general | solution.py:38
  68.0 19.2 %attend.1 = (bf16[1024,768]{1,0:T(8,128)(2,1)S(1)}, f32[1024,768]{1,0:T(8,128)}) custom-call(s32[1]{0:T(128)} %bitcast.flag_ref, bf16[1024,2304]{1,0:T(8,128)(2,1)} %add_convert_fusion.1.q_ref.k_ref.v_ref, bf16[1024,2304]{1,0:T(8,128)(2,1)} %add_convert_fusion.1.q_ref.k_ref.v_ref, bf16[1024,2304]{1,0:T(8,128)(2,1)} %add_convert_fusion.1.q_ref.k_ref.v_ref, ...), custom_call_target="tpu_custom_call" | custom-call | flops 12884901888 | bytes 9437184 | tf_op jit(solution)/shard_map/attend/pallas_call | solution.py:243
  87.2 2.4 all-gather.8.cloned.1.call-done
  89.5 3.4 fusion.68
  93.0 1.6 copy-done.7
  95.0 53.3 %all-gather.10.cloned.1.call-done = bf16[768,3072]{1,0:T(8,128)(2,1)} async-done(((bf16[192,3072]{1,0:T(8,128)(2,1)}), bf16[768,3072]{1,0:T(8,128)(2,1)}) %all-gather.10.cloned.1.call-update) | async-done | bytes 4718608 | tf_op jit(solution)/shard_map/all_gather | solution.py:324
  148.4 37.9 %multiply_convert_fusion = (bf16[1024,3072]{1,0:T(8,128)(2,1)}, f32[1024,3072]{1,0:T(8,128)}, f32[1024,3072]{1,0:T(8,128)}) fusion(f32[3072]{0:T(1024)S(1)} %reshape.254, bf16[768,3072]{1,0:T(8,128)(2,1)} %all-gather.10.cloned.1.call-done, f32[1024,768]{0,1:T(8,128)} %copy-done.7, f32[768]{0:T(1024)S(1)} %reshape.253, f32[768]{0:T(1024)S(1)} %reshape.252, ...), kind=kOutput, calls=%fused_computation.3 | convolution fusion | flops 5043388416 | bytes 39348224 | tf_op jit(solution)/shard_map/dot_general | solution.py:38
  186.3 20.7 %all-gather.12.cloned.1.call-done = bf16[3072,768]{1,0:T(8,128)(2,1)} async-done(((bf16[768,768]{1,0:T(8,128)(2,1)}), bf16[3072,768]{1,0:T(8,128)(2,1)}) %all-gather.12.cloned.1.call-update) | async-done | bytes 4718608 | tf_op jit(solution)/shard_map/all_gather | solution.py:324
  207.0 17.5 %fusion.69 = (bf16[3072]{0:T(1024)(128)(2,1)S(1)}, bf16[1024,3072]{1,0:T(8,128)(2,1)}) fusion(f32[1024,3072]{1,0:T(8,128)} %get-tuple-element.105, bf16[3072,768]{1,0:T(8,128)(2,1)} %all-gather.12.cloned.1.call-done, bf16[1024,768]{0,1:T(8,128)(2,1)S(1)} %copy-done.11, pred[1024]{0:T(1024)(128)(4,1)S(1)} %broadcast_compare_fusion, ...), kind=kOutput, calls=%fused_computation.115 | convolution fusion | flops 4882953216 | bytes 37768192 | tf_op jit(solution)/shard_map/dot_general | solution.py:32
  224.5 9.8 %fusion.70 = (bf16[768]{0:T(1024)(128)(2,1)S(1)}, f32[1024,768]{1,0:T(8,128)}) fusion(bf16[1024,3072]{1,0:T(8,128)(2,1)} %get-tuple-element.130, bf16[768,3072]{1,0:T(8,128)(2,1)} %all-gather.10.cloned.1.call-done), kind=kOutput, calls=%fused_computation.116 | convolution fusion | flops 4832623616 | bytes 14157312 | tf_op jit(solution)/shard_map/dot_general | solution.py:32
  234.3 3.7 copy.74
  237.9 2.9 multiply_reduce_fusion
  240.9 0.9 fusion.64
  244.2 2.6 convolution_convert_fusion.2.do_ref
  246.8 34.4 %attend_back.1 = (bf16[3,1024,768]{2,1,0:T(8,128)(2,1)}, f32[6,2,128]{2,1,0:T(2,128)}) custom-call(s32[1]{0:T(128)} %bitcast.flag_ref, bf16[1024,2304]{1,0:T(8,128)(2,1)} %add_convert_fusion.1.q_ref.k_ref.v_ref, bf16[1024,2304]{1,0:T(8,128)(2,1)} %add_convert_fusion.1.q_ref.k_ref.v_ref, bf16[1024,2304]{1,0:T(8,128)(2,1)} %add_convert_fusion.1.q_ref.k_ref.v_ref, ...), custom_call_target="tpu_custom_call" | custom-call | flops 32212254720 | bytes 14155776 | tf_op jit(solution)/shard_map/attend_back/pallas_call | solution.py:269
  281.3 3.3 fusion.30
  284.6 1.8 fusion.33
  286.4 1.8 fusion.36
  288.1 2.0 pad_maximum_fusion
  290.2 5.8 copy.87
  296.0 1.3 copy-done.4
  297.3 3.9 convolution_convert_fusion.3
  301.3 9.8 %convolution_convert_fusion = bf16[3072,768]{1,0:T(8,128)(2,1)} fusion(bf16[1024,3072]{1,0:T(8,128)(2,1)} %get-tuple-element.104, bf16[1024,768]{0,1:T(8,128)(2,1)} %copy.73, pred[1024]{0:T(1024)(128)(4,1)S(1)} %broadcast_compare_fusion), kind=kOutput, calls=%fused_computation.18 | convolution fusion | flops 4834983936 | bytes 12583936 | tf_op jit(solution)/shard_map/dot_general | solution.py:26
  311.1 9.9 %convolution_convert_fusion.1 = bf16[768,3072]{1,0:T(8,128)(2,1)} fusion(bf16[1024,3072]{1,0:T(8,128)(2,1)} %get-tuple-element.130, f32[1024,768]{0,1:T(8,128)} %copy-done.7, f32[768]{0:T(1024)S(1)} %reshape.253, f32[768]{0:T(1024)S(1)} %reshape.252, f32[1024]{0:T(1024)S(1)} %fusion.53, f32[1024]{0:T(1024)S(1)} %broadcast_multiply_fusion), kind=kOutput, calls=%fused_computation.19 | convolution fusion | flops 4838129664 | bytes 14170112 | tf_op jit(solution)/shard_map/dot_general | solution.py:26
  321.8 3.1 reduce
  325.0 9.3 %select_convert_fusion = bf16[1024,768]{0,1:T(8,128)(2,1)S(1)} fusion(f32[1024,768]{0,1:T(8,128)} %copy-done.7, bf16[1024,3072]{1,0:T(8,128)(2,1)} %get-tuple-element.104, bf16[3072,768]{1,0:T(8,128)(2,1)} %all-gather.12.cloned.1.call-done, f32[768]{0:T(1024)S(1)} %reshape.255, pred[1024]{0:T(1024)(128)(4,1)S(1)} %broadcast_compare_fusion), kind=kOutput, calls=%fused_computation.43 | convolution fusion | flops 4834983936 | bytes 15732736 | tf_op jit(solution)/shard_map/dot_general | solution.py:38
  334.4 1.6 copy.80
  336.6 3.3 fusion.24
  339.9 2.8 fusion.28
  342.8 4.8 fusion.61
  347.7 3.2 fusion.14
  350.9 2.4 copy.88
  353.3 22.0 %reduce-scatter.7.cloned.1.call-done = bf16[192,768]{1,0:T(8,128)(2,1)} async-done(((bf16[768,768]{1,0:T(8,128)(2,1)}), bf16[192,768]{1,0:T(8,128)(2,1)}) %reduce-scatter.7.cloned.1.call-update) | async-done | bytes 294928 | tf_op jit(solution)/shard_map/reduce_scatter | solution.py:319
  375.4 60.0 %reduce-scatter.11.cloned.1.call-done = bf16[768,768]{1,0:T(8,128)(2,1)} async-done(((bf16[3072,768]{1,0:T(8,128)(2,1)}), bf16[768,768]{1,0:T(8,128)(2,1)}) %reduce-scatter.11.cloned.1.call-update) | async-done | bytes 1179664 | tf_op jit(solution)/shard_map/reduce_scatter | solution.py:319
  435.4 60.0 %reduce-scatter.9.cloned.1.call-done = bf16[192,3072]{1,0:T(8,128)(2,1)} async-done(((bf16[768,3072]{1,0:T(8,128)(2,1)}), bf16[192,3072]{1,0:T(8,128)(2,1)}) %reduce-scatter.9.cloned.1.call-update) | async-done | bytes 1179664 | tf_op jit(solution)/shard_map/reduce_scatter | solution.py:319
  495.4 5.5 add_convert_fusion.2
  501.0 2.6 copy.81
  503.6 15.4 %all-reduce.1 = bf16[4,2528]{1,0:T(4,128)(2,1)S(1)} all-reduce(bf16[4,2528]{1,0:T(4,128)(2,1)S(1)} %concatenate.12), channel_id=4, replica_groups=mesh['dp'=8,'fsdp'=4] {'fsdp'}, use_global_device_ids=true, to_apply=%region_21.22.clone | all-reduce | flops 10112 | bytes 40448
  519.7 27.2 %psum.36 = bf16[1,2528]{1,0:T(2,128)(2,1)S(1)} all-reduce(bf16[1,2528]{1,0:T(2,128)(2,1)S(1)} %constant_dynamic-slice_fusion), channel_id=1, replica_groups=mesh['dp'=8,'fsdp'=4] {'dp'}, use_global_device_ids=true, to_apply=%region_22.23 | all-reduce | flops 2528 | bytes 10112 | tf_op jit(solution)/shard_map/psum | solution.py:310
  549.3 40.1 %all-reduce.5.cloned.1.call-done = (bf16[192,2304]{0,1:T(8,128)(2,1)}, bf16[192,768]{1,0:T(8,128)(2,1)}, bf16[192,3072]{1,0:T(8,128)(2,1)}, bf16[768,768]{1,0:T(8,128)(2,1)}) async-done(((bf16[192,2304]{0,1:T(8,128)(2,1)}, bf16[192,768]{1,0:T(8,128)(2,1)}, bf16[192,3072]{1,0:T(8,128)(2,1)}, bf16[768,768]{1,0:T(8,128)(2,1)}), (bf16[192,2304]{0,1:T(8,128)(2,1)}, bf16[192,768]{1,0:T(8,128)(2,1)}, ...) | async-done | bytes 3538960 | tf_op jit(solution)/shard_map/psum | solution.py:320
  589.4 2.6 copy.82
  592.1 0.9 convert_element_type.217
  592.9 1.7 convert_element_type.219
  594.6 1.6 convert_element_type.221
  (167 shorter events, 15.9 us)
Async XLA Ops:
  7.2 3.1 copy-start.35
  7.2 3.0 copy-start.24
  7.2 4.3 copy-start.43
  7.2 4.3 copy-start.42
  7.2 4.3 copy-start.41
  7.2 4.3 copy-start.40
  7.2 4.3 copy-start.39
  7.3 4.3 copy-start.38
  7.3 4.3 copy-start.37
  7.3 4.3 copy-start.34
  7.3 4.3 copy-start.36
  7.3 4.3 copy-start.33
  7.3 52.8 %all-gather.6.cloned.1.call-start = ((), (), s32[]{:S(2)}) async-start(), calls=%async_computation.4 | async-start | bytes 4423680 | tf_op jit(solution)/shard_map/all_gather | solution.py:324
  8.0 81.5 %all-gather.8.cloned.1.call-start = ((), (), s32[]{:S(2)}) async-start(), calls=%async_computation.5 | async-start | bytes 1474560 | tf_op jit(solution)/shard_map/all_gather | solution.py:324
  8.8 139.6 %all-gather.10.cloned.1.call-start = ((), (), s32[]{:S(2)}) async-start(), calls=%async_computation.6 | async-start | bytes 5898240 | tf_op jit(solution)/shard_map/all_gather | solution.py:324
  9.5 197.5 %all-gather.12.cloned.1.call-start = ((), (), s32[]{:S(2)}) async-start(), calls=%async_computation.7 | async-start | bytes 5898240 | tf_op jit(solution)/shard_map/all_gather | solution.py:324
  10.1 340.8 %reduce-scatter.13.cloned.1.call-start = ((), (), s32[]{:S(2)}) async-start(), calls=%async_computation.11 | async-start | bytes 4423680
  32.8 35.2 %copy-start.1 = (f32[1,128]{1,0:T(1,128)}, f32[1,128]{1,0:T(1,128)S(1)}, u32[]{:S(2)}) copy-start(f32[1,128]{1,0:T(1,128)S(1)} %reshape_tile.7.gk_ref) | copy-start | bytes 1540
  33.0 35.0 %copy-start.2 = (f32[1,128]{1,0:T(1,128)}, f32[1,128]{1,0:T(1,128)S(1)}, u32[]{:S(2)}) copy-start(f32[1,128]{1,0:T(1,128)S(1)} %reshape_tile.6.gq_ref) | copy-start | bytes 1540
  33.2 26.9 %copy-start.22 = (f32[768]{0:T(1024)}, f32[768]{0:T(1024)S(1)}, u32[]{:S(2)}) copy-start(f32[768]{0:T(1024)S(1)} %reshape.246) | copy-start | bytes 9220
  33.3 26.8 %copy-start.31 = (f32[768]{0:T(1024)}, f32[768]{0:T(1024)S(1)}, u32[]{:S(2)}) copy-start(f32[768]{0:T(1024)S(1)} %reshape.247) | copy-start | bytes 9220
  33.7 34.3 %copy-start = (s32[1024,1]{1,0:T(8,128)}, s32[1024,1]{1,0:T(8,128)S(1)}, u32[]{:S(2)}) copy-start(s32[1024,1]{1,0:T(8,128)S(1)} %copy.71.seg_ref) | copy-start | bytes 12292
  35.6 24.5 %copy-start.5 = (bf16[1024,768]{0,1:T(8,128)(2,1)}, bf16[1024,768]{0,1:T(8,128)(2,1)S(1)}, u32[]{:S(2)}) copy-start(bf16[1024,768]{0,1:T(8,128)(2,1)S(1)} %copy.70) | copy-start | bytes 4718596
  35.9 32.0 %copy-start.20 = (f32[1024]{0:T(1024)}, f32[1024]{0:T(1024)S(1)}, u32[]{:S(2)}) copy-start(f32[1024]{0:T(1024)S(1)} %broadcast_multiply_fusion.1) | copy-start | bytes 12292
  37.0 31.0 %copy-start.25 = (f32[1024]{0:T(1024)}, f32[1024]{0:T(1024)S(1)}, u32[]{:S(2)}) copy-start(f32[1024]{0:T(1024)S(1)} %fusion.52) | copy-start | bytes 12292
  87.2 5.8 copy-start.3
  95.0 112.0 %copy-start.11 = (bf16[1024,768]{0,1:T(8,128)(2,1)S(1)}, bf16[1024,768]{0,1:T(8,128)(2,1)}, u32[]{:S(2)}) copy-start(bf16[1024,768]{0,1:T(8,128)(2,1)} %copy.73) | copy-start | bytes 4718596
  234.3 3.7 copy-start.8
  237.9 3.0 copy-start.9
  242.3 1.9 copy-start.44
  243.4 3.3 copy-start.15
  246.8 34.4 %copy-start.6 = (bf16[1024,768]{0,1:T(8,128)(2,1)S(1)}, bf16[1024,768]{0,1:T(8,128)(2,1)}, u32[]{:S(2)}) copy-start(bf16[1024,768]{0,1:T(8,128)(2,1)} %copy-done.5) | copy-start | bytes 4718596
  246.8 34.5 %copy-start.21 = (f32[1024]{0:T(1024)S(1)}, f32[1024]{0:T(1024)}, u32[]{:S(2)}) copy-start(f32[1024]{0:T(1024)} %copy-done.20) | copy-start | bytes 12292
  246.8 34.5 %copy-start.23 = (f32[768]{0:T(1024)S(1)}, f32[768]{0:T(1024)}, u32[]{:S(2)}) copy-start(f32[768]{0:T(1024)} %copy-done.22) | copy-start | bytes 9220
  246.8 34.5 %copy-start.26 = (f32[1024]{0:T(1024)S(1)}, f32[1024]{0:T(1024)}, u32[]{:S(2)}) copy-start(f32[1024]{0:T(1024)} %copy-done.25) | copy-start | bytes 12292
  246.8 34.5 %copy-start.32 = (f32[768]{0:T(1024)S(1)}, f32[768]{0:T(1024)}, u32[]{:S(2)}) copy-start(f32[768]{0:T(1024)} %copy-done.31) | copy-start | bytes 9220
  281.3 3.3 copy-start.14
  296.0 79.4 %reduce-scatter.7.cloned.1.call-start = ((), (), s32[]{:S(2)}) async-start(), calls=%async_computation.8 | async-start | bytes 1474560 | tf_op jit(solution)/shard_map/reduce_scatter | solution.py:319
  301.2 134.2 %reduce-scatter.11.cloned.1.call-start = ((), (), s32[]{:S(2)}) async-start(), calls=%async_computation.10 | async-start | bytes 5898240 | tf_op jit(solution)/shard_map/reduce_scatter | solution.py:319
  311.1 184.3 %reduce-scatter.9.cloned.1.call-start = ((), (), s32[]{:S(2)}) async-start(), calls=%async_computation.9 | async-start | bytes 5898240 | tf_op jit(solution)/shard_map/reduce_scatter | solution.py:319
  321.1 268.3 %all-reduce.5.cloned.1.call-start = ((), (), s32[]{:S(2)}) async-start(), calls=%async_computation.12 | async-start | bytes 7667712 | tf_op jit(solution)/shard_map/psum | solution.py:320
  334.4 1.8 copy-start.30
  336.6 3.3 copy-start.18
  342.8 4.9 copy-start.28
  350.8 144.6 %copy-start.13 = (bf16[1024,768]{0,1:T(8,128)(2,1)S(1)}, bf16[1024,768]{0,1:T(8,128)(2,1)}, u32[]{:S(2)}) copy-start(bf16[1024,768]{0,1:T(8,128)(2,1)} %copy.73) | copy-start | bytes 4718596
  589.4 2.6 copy-start.19
  589.4 3.5 copy-start.17
  589.4 5.2 copy-start.16
  (6 other events, 7.3 us)
Sparse Core Ops, SparseCore 0:
  10.0 50.0 all-gather.5
  61.9 27.5 all-gather.7
  91.4 56.9 all-gather.9
  150.1 56.9 all-gather.11
  296.1 47.1 reduce-scatter.12
  346.6 28.6 reduce-scatter.6
  378.4 56.9 reduce-scatter.10
  438.4 56.9 reduce-scatter.8
  498.6 90.7 all-reduce.4
